TPU v7x, 32 devices: a whole 2x2x4 slice. The times are simulated.
32 devices in a mesh: dp: 4 (over z), fsdp: 8 (over y, x, core).
Axes of the slice: x: 2, y: 2, z: 4, core: 2. Of those that a mesh axis runs over, the one named last changes fastest.
Arguments:
- tokens: bfloat16 [32, 2, 640, 512], P(('dp', 'fsdp')), may hold values from -6 to 6
- parents: int32 [8, 2, 16], replicated, may hold values from -1 to 4, as said below
- norm1_gain: float32 [512], P('fsdp'), may hold values from 0.25 to 1.75
- norm1_bias: float32 [512], P('fsdp'), may hold values from -1.75 to 1.75
- w_query: float32 [512, 512], P('fsdp'), may hold values from -0.25 to 0.25
- w_key: float32 [512, 512], P('fsdp'), may hold values from -0.25 to 0.25
- w_value: float32 [512, 512], P('fsdp'), may hold values from -0.25 to 0.25
- w_output: float32 [512, 512], P('fsdp'), may hold values from -0.75 to 0.75
- output_bias: float32 [512], P('fsdp'), may hold values from -1.75 to 1.75
- norm2_gain: float32 [512], P('fsdp'), may hold values from 0.25 to 1.75
- norm2_bias: float32 [512], P('fsdp'), may hold values from -1.75 to 1.75
- w_inner: float32 [512, 2048], P('fsdp'), may hold values from -0.25 to 0.25
- inner_bias: float32 [2048], P('fsdp'), may hold values from -1.75 to 1.75
- w_outer: float32 [2048, 512], P('fsdp'), may hold values from -0.1875 to 0.1875
- outer_bias: float32 [512], P('fsdp'), may hold values from -1.75 to 1.75
- cotangent: bfloat16 [32, 2, 640, 512], P(('dp', 'fsdp')), may hold values from -12 to 12
Outputs:
- layer_out: bfloat16 [32, 2, 640, 512], P(('dp', 'fsdp'))
- grad_tokens: bfloat16 [32, 2, 640, 512], P(('dp', 'fsdp'))
- grad_norm1_gain: float32 [512], P('fsdp')
- grad_norm1_bias: float32 [512], P('fsdp')
- grad_w_query: float32 [512, 512], P('fsdp')
- grad_w_key: float32 [512, 512], P('fsdp')
- grad_w_value: float32 [512, 512], P('fsdp')
- grad_w_output: float32 [512, 512], P('fsdp')
- grad_output_bias: float32 [512], P('fsdp')
- grad_norm2_gain: float32 [512], P('fsdp')
- grad_norm2_bias: float32 [512], P('fsdp')
- grad_w_inner: float32 [512, 2048], P('fsdp')
- grad_inner_bias: float32 [2048], P('fsdp')
- grad_w_outer: float32 [2048, 512], P('fsdp')
- grad_outer_bias: float32 [512], P('fsdp')
Inputs may be any that keep to these rules, and one draw needn't show every extreme that they name: `parents`: for every tree, column 0 (the trunk) and columns 13 to 15 hold -1, columns 1 to 4 (the branches) hold 0, and columns 5 to 12 (the leaves) name the branches 1 to 4, each exactly twice.
All inputs are finite; a program needn't handle non-finite values.
Results may differ from a plain program's by a relative error of at most 0.019.
Values may be sent and summed in bfloat16 or wider, within the bound.
A program may use at most 320 MiB of HBM per device.

v0:
```python
import functools
import math

import jax
import jax.numpy as jnp
import ml_dtypes
import numpy as np
from jax import lax
from jax.experimental import pallas as pl
from jax.experimental.pallas import tpu as pltpu
from jax.sharding import PartitionSpec as P

H = 8
T = 256
f32, bf16 = jnp.float32, jnp.bfloat16
VM = pl.BlockSpec(memory_space=pltpu.VMEM)
SM = pl.BlockSpec(memory_space=pltpu.SMEM)


def mm(a, b):
    return jnp.dot(a, b, preferred_element_type=f32)


def mm_tn(a, b):
    return lax.dot_general(a, b, (((0,), (0,)), ((), ())), preferred_element_type=f32)


def mm_nt(a, b):
    return lax.dot_general(a, b, (((1,), (1,)), ((), ())), preferred_element_type=f32)


def iota(shape, dim):
    return lax.broadcasted_iota(jnp.int32, shape, dim)


def chosen(par, read):
    out = read(0)
    for b in range(1, 4):
        out = jnp.where(par == b + 1, read(b), out)
    return out


def attend(heads, seg, parents_ref, kaug_ref, qT_ref, vT_ref, oT_ref, lse_ref, s_scr, between):
    trunk = 8 * seg
    ntr = trunk // T
    vr = vT_ref.shape[0] // heads
    causal_t = iota((T, T), 0) <= iota((T, T), 1)
    causal_b = iota((seg, seg), 0) <= iota((seg, seg), 1)

    def finish(h, cols, m, acc):
        l = acc[64:65, :]
        oT_ref[pl.ds(pl.multiple_of(h * 64, 64), 64), cols] = (acc[:64] / l).astype(bf16)
        lse_ref[pl.ds(pl.multiple_of(h * 8, 8), 8), cols] = jnp.broadcast_to(m + jnp.log(l), (8, T))

    def head(h, _):
        between(h)
        hk = pl.ds(pl.multiple_of(h * 128, 128), 128)
        hv = pl.ds(pl.multiple_of(h * vr, vr), vr)

        def keys(blk, n):
            return kaug_ref[pl.ds(blk, n), :, hk].reshape(n * seg, 128)

        def full_scores(q, n):
            m = None
            for c in range(n):
                s = mm(keys(2 * c, 2), q)
                s_scr[c * T:(c + 1) * T, :] = s
                cm = jnp.max(s, axis=0, keepdims=True)
                m = cm if m is None else jnp.maximum(m, cm)
            return m

        def full_mix(m, n, acc):
            for c in range(n):
                p = jnp.exp(s_scr[c * T:(c + 1) * T, :] - m).astype(bf16)
                t = mm(vT_ref[hv, c * T:(c + 1) * T], p)
                acc = t if acc is None else acc + t
            return acc

        for t in range(ntr):
            cols = slice(t * T, (t + 1) * T)
            q = qT_ref[hk, cols]
            sd = jnp.where(causal_t, mm(keys(2 * t, 2), q), -1e30)
            m = jnp.max(sd, axis=0, keepdims=True)
            if t:
                m = jnp.maximum(m, full_scores(q, t))
            acc = mm(vT_ref[hv, cols], jnp.exp(sd - m).astype(bf16))
            acc = full_mix(m, t, acc)
            finish(h, cols, m, acc)

        def tail_tile(i, leaf):
            b0 = 8 + 2 * i
            cols = pl.ds(pl.multiple_of(b0 * seg, T), T)
            q = qT_ref[hk, cols]
            rows = []
            for half in range(2):
                rows.append([b0 + half])
                if leaf:
                    rows[-1].append(parents_ref[b0 + half - 7])
            m = full_scores(q, ntr)
            ext = []
            for e in range(len(rows[0])):
                pieces = []
                for half in range(2):
                    kk = keys(rows[half][0], 1) if e == 0 else chosen(rows[half][1], lambda b: keys(8 + b, 1))
                    s = mm(kk, q[:, half * seg:(half + 1) * seg])
                    if e == 0:
                        s = jnp.where(causal_b, s, -1e30)
                    pieces.append(s)
                s = jnp.concatenate(pieces, axis=1)
                m = jnp.maximum(m, jnp.max(s, axis=0, keepdims=True))
                ext.append(s)
            acc = None
            for e in range(len(ext)):
                p = jnp.exp(ext[e] - m).astype(bf16)
                t = []
                for half in range(2):
                    if e == 0:
                        vv = vT_ref[hv, pl.ds(pl.multiple_of(rows[half][0] * seg, seg), seg)]
                    else:
                        vv = chosen(rows[half][1], lambda b: vT_ref[hv, (8 + b) * seg:(9 + b) * seg])
                    t.append(mm(vv, p[:, half * seg:(half + 1) * seg]))
                t = jnp.concatenate(t, axis=1)
                acc = t if acc is None else acc + t
            acc = full_mix(m, ntr, acc)
            finish(h, cols, m, acc)

        lax.fori_loop(0, 2, lambda i, c: (tail_tile(i, False), c)[1], 0)
        lax.fori_loop(2, 6, lambda i, c: (tail_tile(i, True), c)[1], 0)
        return 0

    lax.fori_loop(0, heads, head, 0)


def attend_back(heads, seg, parents_ref, kaug_ref, v_ref, qT_ref, doT_ref, kT_ref, do_ref, qn_ref,
                oT_ref, lse_ref, dqT_ref, dqkv_ref, accK, accV, hook):
    ntr = 8 * seg // T
    causal_t = iota((T, T), 0) <= iota((T, T), 1)
    causal_b = iota((seg, seg), 0) <= iota((seg, seg), 1)
    low_rows = iota((128, T), 0) < 64
    low_lanes = iota((T, 128), 1) < 64

    def pair(pr, _):
        hook("start", pr)
        lanes = pl.ds(pl.multiple_of(pr * 128, 128), 128)
        hk = [pl.ds(pl.multiple_of(pr * 256 + 128 * e, 128), 128) for e in range(2)]
        h64 = [pl.ds(pl.multiple_of(pr * 128 + 64 * e, 64), 64) for e in range(2)]
        accK[...] = jnp.zeros_like(accK)
        accV[...] = jnp.zeros_like(accV)

        def stack(x):
            z = jnp.zeros_like(x)
            return jnp.concatenate([jnp.where(low_lanes, x, z), jnp.where(low_lanes, z, x)], axis=0)

        def prep(cols):
            doT = doT_ref[lanes, cols]
            z = jnp.zeros_like(doT)
            prod = doT.astype(f32) * oT_ref[lanes, cols].astype(f32)
            q, do, lse, delta = [], [], [], []
            for e in range(2):
                q.append(qT_ref[hk[e], cols])
                do.append(jnp.where(low_rows, doT, z) if e == 0 else jnp.where(low_rows, z, doT))
                at = pl.multiple_of((pr * 2 + e) * 8, 8)
                lse.append(jnp.max(lse_ref[pl.ds(at, 8), cols], axis=0, keepdims=True))
                delta.append(jnp.sum(prod[64 * e:64 * e + 64], axis=0, keepdims=True))
            return q, do, lse, delta, stack(do_ref[cols, lanes]), stack(qn_ref[cols, lanes])

        def piece(blk, n, sl, args, mask, par=None):
            q, do, lse, delta, rv, rk = args
            ps, dss, dq = [], [], []

            def rows_of(ref, at):
                if par is None:
                    return ref[pl.ds(blk, n), :, at].reshape(n * seg, 128)
                return chosen(par, lambda b: ref[8 + b, :, at])

            vv = rows_of(v_ref, lanes)
            for e in range(2):
                kk = rows_of(kaug_ref, hk[e])
                p = jnp.exp(mm(kk, q[e][:, sl]) - lse[e][:, sl])
                if mask is not None:
                    p = jnp.where(mask, p, 0.0)
                dp = mm(vv, do[e][:, sl])
                ds = (p * (dp - delta[e][:, sl])).astype(bf16)
                if par is None:
                    kT = kT_ref[h64[e], pl.ds(pl.multiple_of(blk * seg, seg), n * seg)]
                else:
                    kT = chosen(par, lambda b: kT_ref[h64[e], (8 + b) * seg:(9 + b) * seg])
                dq.append(mm(kT, ds))
                ps.append(p.astype(bf16))
                dss.append(ds)
            if sl.stop - sl.start != T:
                rv = jnp.concatenate([rv[sl], rv[T + sl.start:T + sl.stop]], axis=0)
                rk = jnp.concatenate([rk[sl], rk[T + sl.start:T + sl.stop]], axis=0)
            av = mm(jnp.concatenate(ps, axis=1), rv)
            ak = mm(jnp.concatenate(dss, axis=1), rk)
            if par is None:
                accV[pl.ds(blk, n)] += av.reshape(n, seg, 128)
                accK[pl.ds(blk, n)] += ak.reshape(n, seg, 128)
            else:
                for b in range(4):
                    here = jnp.where(par == b + 1, 1.0, 0.0)
                    accK[8 + b] += ak * here
                    accV[8 + b] += av * here
            return dq

        def emit(cols, dq):
            for e in range(2):
                dqT_ref[64 * e:64 * e + 64, cols] = (dq[e] * 0.125).astype(bf16)

        full = slice(0, T)
        for t in range(ntr):
            cols = slice(t * T, (t + 1) * T)
            args = prep(cols)
            dq = piece(2 * t, 2, full, args, causal_t)
            for c in range(t):
                dq = [a + b for a, b in zip(dq, piece(2 * c, 2, full, args, None))]
            emit(cols, dq)

        def tail_tile(i, leaf):
            b0 = 8 + 2 * i
            cols = pl.ds(pl.multiple_of(b0 * seg, T), T)
            args = prep(cols)
            halves = []
            for half in range(2):
                sl = slice(half * seg, (half + 1) * seg)
                d = piece(b0 + half, 1, sl, args, causal_b)
                if leaf:
                    par = parents_ref[b0 + half - 7]
                    d = [x + y for x, y in zip(d, piece(8, 1, sl, args, None, par))]
                halves.append(d)
            dq = [jnp.concatenate([halves[0][e], halves[1][e]], axis=1) for e in range(2)]
            for c in range(ntr):
                dq = [a + b for a, b in zip(dq, piece(2 * c, 2, full, args, None))]
            emit(cols, dq)

        hook("mid", pr)
        lax.fori_loop(0, 2, lambda i, c: (tail_tile(i, False), c)[1], 0)
        hook("late", pr)
        lax.fori_loop(2, 6, lambda i, c: (tail_tile(i, True), c)[1], 0)
        first = pr * 384

        def put(i, x):
            dqkv_ref[:, :, pl.ds(pl.multiple_of(first + 128 * i, 128), 128)] = x

        put(0, dqT_ref[...].T.reshape(20, seg, 128))
        put(1, accK[...].astype(bf16))
        put(2, accV[...].astype(bf16))
        hook("end", pr)
        return 0

    lax.fori_loop(0, heads // 2, pair, 0)


class Dense:
    def __init__(self, rows, width, oF_ref, dy_ref, woi_ref, wu_ref, rows_ref, dxl_ref, dx2_ref, g1_ref, vin_ref,
                 a2s, gs, dus):
        self.__dict__.update({k: v for k, v in locals().items() if k != "self"})
        self.hidden = wu_ref.shape[0]
        self.tiles = self.hidden // width

    def chunk(self, start, x, y_ref):
        width, rows_ref, vin_ref = self.width, self.rows_ref, self.vin_ref
        woi_ref, wu_ref = self.woi_ref, self.wu_ref
        c1 = math.sqrt(2.0 / math.pi)
        c2 = c1 * 0.044715

        def vector(i):
            return rows_ref[0:1, i * width:(i + 1) * width]

        def add_sum(i, x):
            vin_ref[i:i + 1, :] += jnp.sum(x, axis=0, keepdims=True)

        at = pl.ds(pl.multiple_of(start, 128), x.shape[0])
        x2 = fold(x) + mm_tn(self.oF_ref[:, at], woi_ref[:, 0:width]) + vector(2)
        centred = x2 - jnp.mean(x2, axis=-1, keepdims=True)
        inv = lax.rsqrt(jnp.mean(centred * centred, axis=-1, keepdims=True) + 1e-06)
        unit = centred * inv
        a2 = (unit * vector(3) + vector(4)).astype(bf16)
        self.a2s[at, :] = a2
        dy = self.dy_ref[start // x.shape[0]]
        y = x2 + vector(5)
        da2 = None
        for t in range(self.tiles):
            ft = slice(t * width, (t + 1) * width)
            wt = slice(width + t * width, width + (t + 1) * width)
            u = mm(a2, woi_ref[:, wt]) + rows_ref[0:1, 6 * width + t * width:6 * width + (t + 1) * width]
            uu = u * u
            th = jnp.tanh(u * (c1 + c2 * uu))
            p = 0.5 + 0.5 * th
            g = (u * p).astype(bf16)
            slope = p + u * (0.5 - 0.5 * th * th) * (c1 + 3.0 * c2 * uu)
            self.gs[at, ft] = g
            y = y + mm(g, wu_ref[ft, :])
            du = (mm_nt(dy, wu_ref[ft, :]) * slope).astype(bf16)
            self.dus[at, ft] = du
            add_sum(6 + t, fold(du))
            d = mm_nt(du, woi_ref[:, wt])
            da2 = d if da2 is None else da2 + d
        y_ref[...] = y.astype(bf16)
        dyf = fold(dy)
        dn = da2 * vector(3)
        m1 = jnp.mean(dn, axis=-1, keepdims=True)
        m2 = jnp.mean(dn * unit, axis=-1, keepdims=True)
        dx2 = dyf + (dn - m1 - unit * m2) * inv
        dxl = dx2.astype(bf16)
        self.dx2_ref[at, :] = dx2
        self.dxl_ref[at, :] = dxl
        add_sum(2, fold(dxl))
        add_sum(3, da2 * unit)
        add_sum(4, da2)
        add_sum(5, dyf)

    def gradients(self, F):
        width, hidden, tiles, g1_ref = self.width, self.hidden, self.tiles, self.g1_ref
        r, ru = width // F, hidden // F
        nb = T // ru
        dy = self.dy_ref[...].reshape(2 * self.rows, width)

        def outer(t, c):
            val = mm_tn(self.gs[:, pl.ds(pl.multiple_of(t * T, T), T)], dy).astype(bf16)
            g1_ref[pl.ds(t * nb, nb), 0:ru, :] = val.reshape(nb, ru, width)
            return c

        lax.fori_loop(0, hidden // T, outer, 0)
        a2T = self.a2s[...].T
        for t in range(tiles):
            val = mm(a2T, self.dus[:, t * width:(t + 1) * width]).astype(bf16)
            g1_ref[:, ru + t * r:ru + (t + 1) * r, :] = val.reshape(F, r, width)
        val = mm(self.oF_ref[...], self.dxl_ref[...]).astype(bf16)
        g1_ref[:, ru + tiles * r:ru + (tiles + 1) * r, :] = val.reshape(F, r, width)


def slope_parts(head, head_count, length):
    x = np.float32(2.0 ** (2.0 - 4.0 * head / head_count) / length)
    out = []
    for _ in range(3):
        low = np.float32(ml_dtypes.bfloat16(x))
        out.append(float(low))
        x = np.float32(x - low)
    return out


def remote(src, dst, send_sem, recv_sem, target):
    return pltpu.make_async_remote_copy(
        src_ref=src, dst_ref=dst, send_sem=send_sem, recv_sem=recv_sem,
        device_id={"fsdp": target}, device_id_type=pl.DeviceIdType.MESH)


def where_am_i(F):
    f = lax.axis_index("fsdp")
    place = lax.rem(f + 2, F)
    part = lax.rem(place, 4)
    half = part // 2
    core = lax.rem(f, 2)
    base = place - part
    partner = lax.rem(base + lax.rem(part + 2, 4) + F - 2, F)
    sibling = f + 1 - 2 * core
    return f, part, half, core, partner, sibling


def greet(F, f, core, sibling):
    barrier = pltpu.get_barrier_semaphore()
    for d in range(1, F // 2):
        pl.semaphore_signal(barrier, inc=1, device_id={"fsdp": lax.rem(f + 2 * d, F)},
                            device_id_type=pl.DeviceIdType.MESH)
    pl.semaphore_signal(barrier, inc=1, device_id={"fsdp": sibling}, device_id_type=pl.DeviceIdType.MESH)
    pl.semaphore_wait(barrier, F // 2)


def first_kernel(F, n, parents_ref, tok_ref, cot_ref, wq_ref, wk_ref, wv_ref, wo_ref, wi_ref, wu_ref, vec_ref,
                 a1T_out, kaug_out, v_out, kT_out, qn_out, qT_out, oT_out, lse_out, wc_out, wo_out, xs_out, dxl_out,
                 dx2_out, g1_out, lo_ref, vin_ref, rows_ref,
                 xt_ref, a1T_ref, kaug_ref, v_ref, kT_ref, qn_ref, qT_ref, oT_ref, lse_ref, oF_ref, dy_ref,
                 wqkv_ref, woi_ref, wuf_ref, wc, dxl_ref, dx2_ref, g1_ref, a2s, gs, dus,
                 vecs, vT_scr, s_scr, tsend, trecv, gsend, grecv, osem):
    f, part, half, core, partner, sibling = where_am_i(F)
    rows, width = tok_ref.shape[1:]
    seg = rows // 5
    heads = H // 2
    hw = heads * 64
    tree = 4 * rows
    r = wq_ref.shape[0]
    ru = wu_ref.shape[0]
    part1 = part + 1 - 2 * core
    part2 = lax.rem(part + 2, 4)
    part3 = lax.rem(part1 + 2, 4)

    own = pl.ds(pl.multiple_of(f * r, r), r)
    ownu = pl.ds(pl.multiple_of(f * ru, ru), ru)
    vecs[f] = vec_ref[...]
    wqkv_ref[own, 0:width] = wq_ref[...].astype(bf16)
    wqkv_ref[own, width:2 * width] = wk_ref[...].astype(bf16)
    wqkv_ref[own, 2 * width:3 * width] = wv_ref[...].astype(bf16)

    greet(F, f, core, sibling)

    def slot(g, src):
        if g == 0:
            return vecs.at[src]
        if g == 3:
            return wuf_ref.at[pl.ds(pl.multiple_of(src * ru, ru), ru)]
        ref = wqkv_ref if g == 1 else woi_ref
        return ref.at[pl.ds(pl.multiple_of(src * r, r), r)]

    def direct(g, d):
        return remote(slot(g, f), slot(g, f), gsend.at[g, d], grecv.at[g, d],
                      sibling if d == 0 else lax.rem(f + 2 * d, F))

    def came(g, d):
        src = sibling if d == 0 else lax.rem(f + F - 2 * d, F)
        remote(slot(g, src), slot(g, src), gsend.at[g, d], grecv.at[g, d], sibling).wait_recv()

    def forward(g, d):
        src = lax.rem(f + F - 2 * d, F)
        return remote(slot(g, src), slot(g, src), gsend.at[g, F // 2 + d], grecv.at[g, F // 2 + d], sibling)

    def forwarded(g, d):
        src = lax.rem(sibling + F - 2 * d, F)
        remote(slot(g, src), slot(g, src), gsend.at[g, F // 2 + d], grecv.at[g, F // 2 + d], sibling).wait_recv()

    chips = range(1, F // 2)

    def send_all(g):
        for d in range(F // 2):
            direct(g, d).start()

    def pass_on(g):
        for d in chips:
            came(g, d)
            forward(g, d).start()

    def receive_rest(g):
        came(g, 0)
        for d in chips:
            forwarded(g, d)

    x_out = remote(tok_ref.at[1 - half], xt_ref.at[part], tsend.at[0], trecv.at[0], partner)
    x_sib = remote(tok_ref.at[half], xt_ref.at[part], tsend.at[1], trecv.at[1], sibling)
    x_fwd = remote(xt_ref.at[part2], xt_ref.at[part2], tsend.at[2], trecv.at[2], sibling)
    dy_out = remote(cot_ref.at[1 - half], dy_ref.at[half], tsend.at[3], trecv.at[3], partner)
    dy_own = pltpu.make_async_copy(cot_ref.at[half], dy_ref.at[half], tsend.at[4])

    send_all(0)
    send_all(1)
    x_out.start()
    x_sib.start()
    dy_own.start()
    xt_ref[part] = tok_ref[half]
    woi_ref[own, 0:width] = wo_ref[...].astype(bf16)
    woi_ref[own, width:] = wi_ref[...].astype(bf16)
    wuf_ref[ownu, :] = wu_ref[...].astype(bf16)
    pass_on(0)
    pass_on(1)
    receive_rest(0)

    table = jnp.max(vecs[...], axis=1).astype(bf16)
    words = table.shape[1]

    def vector_row(first, m, length):
        col = iota((words, length), 1)
        pick = iota((words, length), 0) == first + (col & (m - 1))
        spread = mm(table, pick.astype(bf16))
        shift = m.bit_length() - 1
        mine = iota((F, length), 0) == (iota((F, length), 1) >> shift)
        return jnp.sum(jnp.where(mine, spread, 0.0), axis=0, keepdims=True)

    def all_rows(first, last):
        for i in range(first, last):
            rows_ref[:, i * width:(i + 1) * width] = jnp.broadcast_to(vector_row(i * n, n, width), (8, width))

    all_rows(0, 2)
    hidden = rows_ref.shape[1] - 6 * width
    receive_rest(1)

    lane = iota((seg, 128), 1)
    offs = iota((seg, 128), 0)
    arow = iota((64, rows), 0)

    def project(p):
        x = xt_ref[p].astype(f32)
        gain = rows_ref[0:1, 0:width]
        shift = rows_ref[0:1, width:2 * width]
        mean = jnp.mean(x, axis=-1, keepdims=True)
        x = x - mean
        inv = lax.rsqrt(jnp.mean(x * x, axis=-1, keepdims=True) + 1e-06)
        a1 = (x * inv * gain + shift).astype(bf16)

        def proj(i):
            return mm(a1, wqkv_ref[:, pl.ds(pl.multiple_of(i * width + core * hw, hw), hw)])

        cols = pl.ds(pl.multiple_of(p * rows, rows), rows)
        a1T_ref[:, cols] = a1.T
        q = (proj(0) * 0.125).astype(bf16)
        qn_ref[cols, :] = q
        qT = q.T
        k = proj(1).astype(bf16)
        kT_ref[:, cols] = k.T
        v = proj(2).astype(bf16)
        v_ref[pl.ds(p * 5, 5)] = v.reshape(5, seg, hw)
        vT = v.T
        for h in range(heads):
            a, b = slope_parts(h, H, tree), slope_parts(heads + h, H, tree)
            aug = jnp.zeros((64, rows), f32)
            for j in range(3):
                s = jnp.where(core == 0, a[j], b[j])
                aug = jnp.where((arow == j) | (arow == j + 3), s, aug)
            aug = aug.astype(bf16)
            lo, hi = 128 * h + 64 * (h % 2), 128 * h + 64 - 64 * (h % 2)
            qT_ref[lo:lo + 64, cols] = qT[64 * h:64 * h + 64]
            qT_ref[hi:hi + 64, cols] = aug
            vT_scr[80 * h:80 * h + 64, cols] = vT[64 * h:64 * h + 64]
            vT_scr[80 * h + 64:80 * h + 80, cols] = jnp.ones((16, rows), bf16)
        for b in range(5):
            blk = p * 5 + b
            start = jnp.where(blk < 8, blk * seg, jnp.where(blk < 12, 8 * seg, 9 * seg))
            spot = offs + start
            hi = (spot & -8).astype(f32)
            lo = (spot & 7).astype(f32)
            for h in range(heads):
                at = 64 - 64 * (h % 2)
                l = lane - at
                aug = jnp.where((l >= 0) & (l < 3), hi, jnp.where((l >= 3) & (l < 6), lo, 0.0)).astype(bf16)
                keep = (lane < 64) if h % 2 == 0 else (lane >= 64)
                kk = k[b * seg:(b + 1) * seg, 128 * (h // 2):128 * (h // 2) + 128]
                kaug_ref[blk, :, 128 * h:128 * h + 128] = jnp.where(keep, kk, aug)

    x_sib.wait_recv()

    def visit(i, c):
        @pl.when(i == 1)
        def _():
            all_rows(2, 6)
            rows_ref[:, 6 * width:] = jnp.broadcast_to(vector_row(6 * n, hidden // F, hidden), (8, hidden))
            x_out.wait_recv()
            x_fwd.start()
            send_all(2)
            send_all(3)
            dy_out.start()

        @pl.when(i == 3)
        def _():
            x_fwd.wait_recv()

        project(jnp.where(i == 0, part, jnp.where(i == 1, part1, jnp.where(i == 2, part2, part3))))
        return c

    lax.fori_loop(0, 4, visit, 0)
    for i in range(heads // 2):
        for k in range(3):
            src = pl.ds(pl.multiple_of(k * width + core * hw + 128 * i, 128), 128)
            wc[:, 384 * i + 128 * k:384 * i + 128 * k + 128] = wqkv_ref[:, src]

    outs = [(a1T_ref, a1T_out), (kaug_ref, kaug_out), (v_ref, v_out), (kT_ref, kT_out), (qn_ref, qn_out),
            (qT_ref, qT_out), (wc, wc_out), (xt_ref.at[core], xs_out.at[0]), (xt_ref.at[core + 2], xs_out.at[1]),
            (oT_ref, oT_out), (lse_ref, lse_out),
            (woi_ref.at[pl.ds(pl.multiple_of(core * hw, hw), hw), 0:width], wo_out),
            (dxl_ref.at[0:rows], dxl_out.at[0]), (dxl_ref.at[rows:2 * rows], dxl_out.at[1]),
            (dx2_ref.at[0:rows], dx2_out.at[0]), (dx2_ref.at[rows:2 * rows], dx2_out.at[1]), (g1_ref, g1_out)]
    copies = [pltpu.make_async_copy(a, b, osem.at[i]) for i, (a, b) in enumerate(outs)]
    for c in copies[:9]:
        c.start()

    def between(h):
        @pl.when(h == 2)
        def _():
            pass_on(2)

    attend(heads, seg, parents_ref, kaug_ref, qT_ref, vT_scr, oT_ref, lse_ref, s_scr, between)

    other = 1 - core
    sent = []
    for i in range(2):
        cols = pl.ds(pl.multiple_of((other + 2 * i) * rows, rows), rows)
        at = (pl.ds(pl.multiple_of(core * hw, hw), hw), slice(i * rows, (i + 1) * rows))
        c = remote(oT_ref.at[:, cols], oF_ref.at[at], tsend.at[5 + i], trecv.at[5 + i], sibling)
        c.start()
        sent.append(c)
    for i in range(2):
        mine = pl.ds(pl.multiple_of((core + 2 * i) * rows, rows), rows)
        at = (pl.ds(pl.multiple_of(core * hw, hw), hw), slice(i * rows, (i + 1) * rows))
        oF_ref[at] = oT_ref[:, mine]
    copies[9].start()
    copies[10].start()
    receive_rest(2)
    copies[11].start()
    pass_on(3)
    for c in sent:
        c.wait_recv()
    receive_rest(3)
    dy_own.wait()

    vin_ref[...] = jnp.zeros_like(vin_ref)
    dense = Dense(rows, width, oF_ref, dy_ref, woi_ref, wuf_ref, rows_ref, dxl_ref, dx2_ref, g1_ref, vin_ref,
                  a2s, gs, dus)
    y_out = remote(xt_ref.at[other + 2 * (1 - half)], lo_ref.at[half],
                   tsend.at[7], trecv.at[7], partner)
    keep_y = pltpu.make_async_copy(xt_ref.at[other + 2 * half], lo_ref.at[half], osem.at[17])

    def dense_step(s, c):
        i = jnp.where(s == 0, half, 1 - half)

        @pl.when(s == 1)
        def _():
            keep_y.start()
            dy_out.wait_recv()

        dense.chunk(i * rows, xt_ref[core + 2 * i], xt_ref.at[other + 2 * i])
        return c

    lax.fori_loop(0, 2, dense_step, 0)
    y_out.start()
    for c in copies[12:16]:
        c.start()
    dense.gradients(F)
    copies[16].start()
    for c in copies:
        c.wait()
    keep_y.wait()
    y_out.wait()
    dy_out.wait_send()
    x_out.wait_send()
    x_sib.wait_send()
    x_fwd.wait_send()
    for c in sent:
        c.wait_send()
    for g in range(4):
        for d in range(F // 2):
            direct(g, d).wait_send()
        for d in chips:
            forward(g, d).wait_send()


def first(F, parents, tokens, cotangent, weights, vec, n):
    _, rows, width = tokens.shape
    tree = 4 * rows
    heads = H // 2
    hw = heads * 64
    seg = rows // 5
    hidden = weights[4].shape[1]
    r, ru = width // F, hidden // F
    R1 = ru + (hidden // width + 1) * r
    two = 2 * rows
    keep = [((width, tree), bf16), ((20, seg, heads * 128), bf16), ((20, seg, hw), bf16), ((hw, tree), bf16),
            ((tree, hw), bf16), ((heads * 128, tree), bf16), ((hw, tree), bf16), ((heads * 8, tree), f32)]
    out = keep + [((width, 3 * hw), bf16), ((hw, width), bf16), ((2, rows, width), bf16), ((2, rows, width), bf16),
                  ((2, rows, width), f32), ((F, R1, width), bf16), ((2, rows, width), bf16),
                  ((16, width), f32), ((8, 6 * width + hidden), f32)]
    scratch = [((4, rows, width), bf16)] + keep + [
        ((2 * hw, two), bf16), ((2, rows, width), bf16), ((width, 3 * width), bf16), ((width, width + hidden), bf16),
        ((hidden, width), bf16), ((width, 3 * hw), bf16), ((two, width), bf16),
        ((two, width), f32), ((F, R1, width), bf16), ((two, width), bf16), ((two, hidden), bf16),
        ((two, hidden), bf16), ((F,) + vec.shape, f32), ((heads * 80, tree), bf16), ((8 * seg, T), f32)]
    ANY = pl.BlockSpec(memory_space=pl.ANY)
    dma = pltpu.SemaphoreType.DMA
    return pl.pallas_call(
        functools.partial(first_kernel, F, n),
        out_shape=[jax.ShapeDtypeStruct(s, d) for s, d in out],
        in_specs=[SM, VM, ANY] + [VM] * 7,
        out_specs=[ANY] * 15 + [VM] * 2,
        scratch_shapes=[pltpu.VMEM(s, d) for s, d in scratch] + [
            dma((8,)), dma((8,)), dma((4, F)), dma((4, F)), dma((18,))],
        name="front",
        compiler_params=pltpu.CompilerParams(vmem_limit_bytes=64 << 20, collective_id=0, has_side_effects=True),
    )(parents, tokens, cotangent, *weights, vec)


def fold(x):
    return x.astype(f32)


class Chain:
    def __init__(self, F, f, sums, got, block, zgot, final, send, recv):
        self.F, self.f, self.sums, self.got, self.block = F, f, sums, got, block
        self.zgot, self.final, self.send, self.recv = zgot, final, send, recv
        self.chip = f // 2
        self.chips = F // 2
        self.planes = lax.axis_size("dp")
        self.plane = lax.axis_index("dp")
        self.rows = sums.shape[1]
        self.zrows = block.shape[0] // self.planes

    def _b(self, d):
        return remote(self.sums.at[lax.rem(self.chip + d, self.chips)], self.got.at[d - 1],
                      self.send.at[d], self.recv.at[d], lax.rem(self.f + 2 * d, self.F))

    def _chunk(self, z):
        return pl.ds(pl.multiple_of(z * self.zrows, 16), self.zrows)

    def _c(self, e):
        z = lax.rem(self.plane + e, self.planes)
        i = self.chips + e
        return pltpu.make_async_remote_copy(
            src_ref=self.block.at[self._chunk(z)], dst_ref=self.zgot.at[e - 1],
            send_sem=self.send.at[i], recv_sem=self.recv.at[i],
            device_id={"dp": z}, device_id_type=pl.DeviceIdType.MESH)

    def _d(self, e, src=None):
        z = lax.rem(self.plane + e, self.planes)
        i = self.chips + self.planes + e
        here = self._chunk(self.plane if src is None else src)
        return pltpu.make_async_remote_copy(
            src_ref=self.final.at[here], dst_ref=self.final.at[here],
            send_sem=self.send.at[i], recv_sem=self.recv.at[i],
            device_id={"dp": z}, device_id_type=pl.DeviceIdType.MESH)

    def start_plane(self):
        for d in range(1, self.chips):
            self._b(d).start()

    def start_z(self):
        for d in range(1, self.chips):
            self._b(d).wait_recv()
        total = fold(self.sums[self.chip])
        for d in range(1, self.chips):
            total = total + fold(self.got[d - 1])
        self.block[0:self.rows] = total.astype(bf16)
        for e in range(1, self.planes):
            self._c(e).start()

    def start_back(self):
        for e in range(1, self.planes):
            self._c(e).wait_recv()
        here = self._chunk(self.plane)
        total = fold(self.block[here])
        for e in range(1, self.planes):
            total = total + fold(self.zgot[e - 1])
        self.final[here] = total.astype(bf16)
        for e in range(1, self.planes):
            self._d(e).start()

    def receive(self):
        for e in range(1, self.planes):
            self._d(e, lax.rem(self.plane + self.planes - e, self.planes)).wait_recv()

    def close(self):
        for d in range(1, self.chips):
            self._b(d).wait_send()
        for e in range(1, self.planes):
            self._c(e).wait_send()
            self._d(e).wait_send()


def last_kernel(F, parents_ref, kaug_h, v_h, qT_h, kT_h, qn_h, oT_h, lse_h, a1T_h, wc_h, wo_h, xs_h, dxl_ref, dx2_h,
                g1_ref, vin_ref, n1_ref,
                gt_ref, gq_ref, fin1, vout_ref,
                kaug_ref, v_ref, qT_ref, kT_ref, qn_ref, oT_ref, lse_ref, a1T_ref, wc, wo_scr, xs, dx2s,
                dxs, doT, do, dqT, dqkv, accK, accV, das, dar,
                a_sum, a_got, b_got, blk1, z1, sum2, got2, blk2, z2, fin2,
                vs, vgot, dxo, tsend, trecv, send1, recv1, send2, recv2, vsend, vrecv, lsem):
    f, part, half, core, partner, sibling = where_am_i(F)
    planes = lax.axis_size("dp")
    plane = lax.axis_index("dp")
    heads = H // 2
    hw = heads * 64
    _, rows, width = dxl_ref.shape
    chips = F // 2
    other = 1 - core
    tree = 4 * rows
    seg = rows // 5

    pairs = [(wo_h, wo_scr), (qT_h, qT_ref), (kaug_h, kaug_ref), (v_h, v_ref), (kT_h, kT_ref), (qn_h, qn_ref),
             (oT_h, oT_ref), (lse_h, lse_ref), (g1_ref.at[:, core], a_sum), (a1T_h, a1T_ref), (wc_h, wc), (xs_h, xs),
             (dx2_h, dx2s)]
    loads = [pltpu.make_async_copy(a, b, lsem.at[i]) for i, (a, b) in enumerate(pairs)]
    for c in loads:
        c.start()

    barrier = pltpu.get_barrier_semaphore()
    for d in range(1, chips):
        pl.semaphore_signal(barrier, inc=1, device_id={"fsdp": lax.rem(f + 2 * d, F)},
                            device_id_type=pl.DeviceIdType.MESH)
    for e in range(1, planes):
        pl.semaphore_signal(barrier, inc=1, device_id={"dp": lax.rem(plane + e, planes)},
                            device_id_type=pl.DeviceIdType.MESH)
    pl.semaphore_signal(barrier, inc=1, device_id={"fsdp": sibling}, device_id_type=pl.DeviceIdType.MESH)
    pl.semaphore_wait(barrier, chips + planes - 1)

    dx_sw = remote(dxl_ref, dxs, tsend.at[0], trecv.at[0], sibling)
    a_out = remote(g1_ref.at[:, other], a_got, tsend.at[1], trecv.at[1], sibling)
    dx_sw.start()
    a_out.start()

    def make_do(p, x):
        cols = pl.ds(pl.multiple_of(p * rows, rows), rows)
        d = mm_nt(x, wo_scr[...]).astype(bf16)
        do[cols, :] = d
        doT[:, cols] = d.T

    loads[0].wait()
    lax.fori_loop(0, 2, lambda i, c: (make_do(core + 2 * i, dxl_ref[i]), c)[1], 0)

    one = Chain(F, f, a_sum, b_got, blk1, z1, fin1, send1, recv1)
    loads[8].wait()
    a_out.wait_recv()

    def add_block(j, c):
        a_sum[j] = (fold(a_sum[j]) + fold(a_got[j])).astype(bf16)
        return c

    lax.fori_loop(0, chips, add_block, 0)
    one.start_plane()
    dx_sw.wait_recv()
    lax.fori_loop(0, 2, lambda i, c: (make_do(other + 2 * i, dxs[i]), c)[1], 0)
    for c in loads[1:8] + loads[9:]:
        c.wait()

    def chain(pr):
        return Chain(F, f, sum2.at[pr], got2.at[pr], blk2.at[pr], z2.at[pr], fin2.at[pr], send2.at[pr], recv2.at[pr])

    two = [chain(0), chain(1)]
    r = width // F
    r2 = 2 * r

    def hook(name, pr):
        if name == "mid":
            @pl.when(pr == 1)
            def _():
                one.start_z()
                two[0].start_z()
        if name == "late":
            @pl.when(pr == 1)
            def _():
                one.start_back()
                two[0].start_back()
        if name == "end":
            g = mm(a1T_ref[...], dqkv[:, :, pl.ds(pl.multiple_of(pr * 384, 384), 384)].reshape(tree, 384)).astype(bf16)
            for j in range(chips):
                sum2[pr, j] = g[j * r2:(j + 1) * r2]
            chain(pr).start_plane()

    attend_back(heads, seg, parents_ref, kaug_ref, v_ref, qT_ref, doT, kT_ref, do, qn_ref, oT_ref, lse_ref,
                dqT, dqkv, accK, accV, hook)

    def da1_of(p):
        return mm_nt(dqkv[pl.ds(p * 5, 5)].reshape(rows, 3 * hw), wc[...])

    def da_out(s):
        i = (1 - half) if s == 0 else half
        return remote(das.at[i], dar.at[i], tsend.at[2 + s], trecv.at[2 + s], sibling)

    dx_out = remote(dxo.at[1 - half], gt_ref.at[half], tsend.at[4], trecv.at[4], partner)
    keep_dx = pltpu.make_async_copy(dxo.at[half], gt_ref.at[half], lsem.at[13])
    vs[0] = vin_ref[...]
    row = iota((16, width), 0)

    def finish_rows(s, c):
        i = jnp.where(s == 0, 1 - half, half)
        das[i] = da1_of(other + 2 * i).astype(bf16)
        for k in range(2):
            @pl.when(s == k)
            def _():
                da_out(k).start()
        x = fold(xs[i])
        x = x - jnp.mean(x, axis=-1, keepdims=True)
        inv = lax.rsqrt(jnp.mean(x * x, axis=-1, keepdims=True) + 1e-06)
        unit = x * inv
        da = da1_of(core + 2 * i)
        for k in range(2):
            @pl.when(s == k)
            def _():
                da_out(k).wait_recv()
        da = da + fold(dar[i])
        dn = da * n1_ref[0:1, 0:width]
        m1 = jnp.mean(dn, axis=-1, keepdims=True)
        m2 = jnp.mean(dn * unit, axis=-1, keepdims=True)
        dxo[i] = (dx2s[i] + (dn - m1 - unit * m2) * inv).astype(bf16)
        gs = jnp.sum(da * unit, axis=0, keepdims=True)
        bs = jnp.sum(da, axis=0, keepdims=True)
        vs[0] += jnp.where(row == 0, gs, 0.0) + jnp.where(row == 1, bs, 0.0)

        @pl.when(s == 0)
        def _():
            dx_out.start()

        @pl.when(s == 1)
        def _():
            keep_dx.start()

        return c

    lax.fori_loop(0, 2, finish_rows, 0)
    v_sib = remote(vs.at[0], vgot.at[0], vsend.at[0], vrecv.at[0], sibling)
    v_sib.start()
    two[1].start_z()
    v_sib.wait_recv()
    vs[1] = vs[0] + vgot[0]
    v_chip = [remote(vs.at[1], vgot.at[d], vsend.at[d], vrecv.at[d], lax.rem(f + 2 * d, F)) for d in range(1, chips)]
    for c in v_chip:
        c.start()
    two[1].start_back()
    for c in v_chip:
        c.wait_recv()
    total = vs[1]
    for d in range(1, chips):
        total = total + vgot[d]
    vgot[chips + plane] = total

    def v_z(e, sender):
        return pltpu.make_async_remote_copy(
            src_ref=vgot.at[chips + sender], dst_ref=vgot.at[chips + sender],
            send_sem=vsend.at[chips + e], recv_sem=vrecv.at[chips + e],
            device_id={"dp": lax.rem(plane + e, planes)}, device_id_type=pl.DeviceIdType.MESH)

    for e in range(1, planes):
        v_z(e, plane).start()

    one.receive()
    s_out = []
    for pr in range(2):
        two[pr].receive()
        c = remote(fin2.at[pr, pl.ds(pl.multiple_of(other * r, r), r)], gq_ref.at[core, pr],
                   tsend.at[5 + pr], trecv.at[5 + pr], sibling)
        c.start()
        gq_ref[core, pr] = fin2[pr, pl.ds(pl.multiple_of(core * r, r), r), :]
        s_out.append(c)
    for e in range(1, planes):
        v_z(e, lax.rem(plane + planes - e, planes)).wait_recv()
    total = vgot[chips]
    for z in range(1, planes):
        total = total + vgot[chips + z]
    vout_ref[...] = total
    for c in s_out:
        c.wait()
    dx_out.wait()
    keep_dx.wait()
    one.close()
    for c in two:
        c.close()
    for c in [dx_sw, a_out, v_sib, da_out(0), da_out(1)] + v_chip:
        c.wait_send()
    for e in range(1, planes):
        v_z(e, plane).wait_send()


def last(F, DP, parents, kept, wc, wo, xs, dxl, dx2, g1, vin, rows_vec):
    a1T, kaug, v, kT, qn, qT, oT, lse = kept
    _, rows, width = dxl.shape
    heads = H // 2
    hw = heads * 64
    tree = 4 * rows
    seg = rows // 5
    chips = F // 2
    r = width // F
    R1 = g1.shape[2]
    r2 = 2 * r

    def zrows(n):
        return -(-n // (16 * DP)) * 16

    Z1, Z2 = zrows(R1), zrows(r2)
    ANY = pl.BlockSpec(memory_space=pl.ANY)
    dma = pltpu.SemaphoreType.DMA
    out = [((2, rows, width), bf16), ((2, 2, r, 384), bf16), ((Z1 * DP, width), bf16), ((16, width), f32)]
    big = [kaug, v, qT, kT, qn, oT, lse, a1T, wc, wo, xs]
    scratch = [(a.shape, a.dtype) for a in big] + [
        ((2, rows, width), f32),
        ((2, rows, width), bf16), ((hw, tree), bf16), ((tree, hw), bf16), ((128, tree), bf16),
        ((20, seg, 3 * hw), bf16), ((20, seg, 128), f32), ((20, seg, 128), f32),
        ((2, rows, width), bf16), ((2, rows, width), bf16),
        ((chips, R1, width), bf16), ((chips, R1, width), bf16), ((chips - 1, R1, width), bf16),
        ((Z1 * DP, width), bf16), ((DP - 1, Z1, width), bf16),
        ((2, chips, r2, 384), bf16), ((2, chips - 1, r2, 384), bf16), ((2, Z2 * DP, 384), bf16),
        ((2, DP - 1, Z2, 384), bf16), ((2, Z2 * DP, 384), bf16),
        ((2, 16, width), f32), ((chips + DP, 16, width), f32), ((2, rows, width), bf16),
    ]
    nsem = chips + 2 * DP
    return pl.pallas_call(
        functools.partial(last_kernel, F),
        out_shape=[jax.ShapeDtypeStruct(s, d) for s, d in out],
        in_specs=[SM] + [ANY] * 11 + [VM, ANY, ANY, VM, VM],
        out_specs=[ANY] + [VM] * 3,
        scratch_shapes=[pltpu.VMEM(s, d) for s, d in scratch] + [
            dma((7,)), dma((7,)), dma((nsem,)), dma((nsem,)), dma((2, nsem)), dma((2, nsem)),
            dma((chips + DP,)), dma((chips + DP,)), dma((14,))],
        name="back",
        compiler_params=pltpu.CompilerParams(vmem_limit_bytes=64 << 20, collective_id=1, has_side_effects=True),
    )(parents, *big, dxl, dx2, g1, vin, rows_vec)


def finish_kernel(lo_in, gt_in, fin1, gq, lo_ref, gt_ref, gwq_ref, gwk_ref, gwv_ref, gwo_ref, gwi_ref, gwu_ref):
    lo_ref[...] = lo_in[...]
    gt_ref[...] = gt_in[...]
    r, width = gwo_ref.shape
    ru = gwu_ref.shape[0]
    gwu_ref[...] = fold(fin1[0:ru])
    pieces = gwi_ref.shape[1] // width
    for c in range(pieces):
        gwi_ref[:, c * width:(c + 1) * width] = fold(fin1[ru + c * r:ru + (c + 1) * r])
    gwo_ref[...] = fold(fin1[ru + pieces * r:ru + (pieces + 1) * r])
    for k, ref in enumerate((gwq_ref, gwk_ref, gwv_ref)):
        for c in range(2):
            for pr in range(2):
                at = (2 * c + pr) * 128
                ref[:, at:at + 128] = fold(gq[c, pr, :, 128 * k:128 * k + 128])


def finish(F, lo, gt, fin1, gq, hidden):
    width = lo.shape[2]
    r, ru = width // F, hidden // F
    shapes = [(r, width)] * 4 + [(r, hidden), (ru, width)]
    return pl.pallas_call(
        finish_kernel,
        out_shape=[jax.ShapeDtypeStruct(lo.shape, bf16), jax.ShapeDtypeStruct(gt.shape, bf16)]
        + [jax.ShapeDtypeStruct(s, f32) for s in shapes],
        in_specs=[VM] * 4,
        out_specs=[VM] * 8,
        name="finish",
    )(lo, gt, fin1, gq)


def on_device(tokens, parents, n1g, n1b, wq, wk, wv, wo, ob, n2g, n2b, wi, ib, wu, ub, cotangent):
    F = lax.axis_size("fsdp")
    fi = lax.axis_index("fsdp")
    place = (fi + 2) % F
    half = (place % 4) // 2
    quad = lax.axis_index("dp") * (F // 4) + place // 4
    parent_row = parents[quad, half]
    _, _, rows, width = tokens.shape

    n = n1g.shape[0]
    vec = jnp.concatenate([n1g, n1b, ob, n2g, n2b, ub, ib])
    vec = lax.reduce_precision(vec, 8, 7)
    vec = jnp.broadcast_to(jnp.pad(vec, (0, -vec.shape[0] % 128)), (8, vec.shape[0] + -vec.shape[0] % 128))
    hidden = wi.shape[1]
    ru = hidden // F
    (a1T, kaug, v, kT, qn, qT, oT, lse, wc, wo_own, xs, dxl, dx2, g1, lo, vin, vrows) = first(
        F, parent_row, tokens[0], cotangent[0], (wq, wk, wv, wo, wi, wu), vec, n)
    gt, gq, fin1, vout = last(
        F, lax.axis_size("dp"), parent_row, (a1T, kaug, v, kT, qn, qT, oT, lse), wc, wo_own, xs, dxl, dx2,
        g1.reshape(F // 2, 2, -1, width), vin, vrows)
    lo, gt, gwq, gwk, gwv, gwo, gwi, gwu = finish(F, lo, gt, fin1, gq, hidden)
    sv = lax.dynamic_slice_in_dim(vout[:6], fi * n, n, 1)
    sib = lax.dynamic_slice_in_dim(vout[6:6 + hidden // width].reshape(-1), fi * ru, ru, 0)
    return (lo[None], gt[None], sv[0], sv[1], gwq, gwk, gwv, gwo, sv[2], sv[3], sv[4], gwi, sib, gwu, sv[5])


def solution(mesh):
    tok = P(("dp", "fsdp"), None, None, None)
    v, m = P("fsdp"), P("fsdp", None)
    return jax.shard_map(
        on_device,
        mesh=mesh,
        in_specs=(tok, P(), v, v, m, m, m, m, v, v, v, m, v, m, v, tok),
        out_specs=(tok, tok, v, v, m, m, m, m, v, v, v, m, v, m, v),
        check_vma=False,
    )
```

profile of v0, /device:TPU:0, one launch (start us, length us, event | category | flops | bytes accessed | tf_op | source)
XLA Modules:
  0.0 214.6 jit_solution(11993692863093695570)
XLA Ops:
  0.7 1.2 dynamic-slice_bitcast_fusion.parents_ref
  1.9 0.8 concatenate.3
  2.8 0.6 broadcast_in_dim.9.vec_ref
  3.4 97.0 %front.1 = (bf16[512,2560]{1,0:T(8,128)(2,1)}, bf16[20,128,512]{2,1,0:T(8,128)(2,1)}, bf16[20,128,256]{2,1,0:T(8,128)(2,1)}, bf16[256,2560]{1,0:T(8,128)(2,1)}, ...) custom-call(s32[16]{0:T(128)} %dynamic-slice_bitcast_fusion.parents_, ...), custom_call_target="tpu_custom_call" | custom-call | tf_op jit(solution)/shard_map/front/pallas_call | solution.py:655
  100.4 108.9 %back.1 = (bf16[2,640,512]{2,1,0:T(8,128)(2,1)}, bf16[2,2,64,384]{3,2,1,0:T(8,128)(2,1)}, bf16[576,512]{1,0:T(8,128)(2,1)}, f32[16,512]{1,0:T(8,128)}) custom-call(s32[16]{0:T(128)} %dynamic-slice_bitcast_fusion.parents_ref, bf16[20,128,512]{2,1,0:T(8,128)(2,1)} %get-tuple-element.45.kaug_h, bf16[20,128,256]{2,1,0:T(8,128)(2,1)} %get-tuple-element.46.v_h, ...), custom_call_target="tpu_custom_call" | custom-call | tf_op jit(solution)/shard_map/back/pallas_call | solution.py:967
  209.3 0.0 copy-start
  209.4 4.0 %finish.1 = (bf16[2,640,512]{2,1,0:T(8,128)(2,1)}, bf16[2,640,512]{2,1,0:T(8,128)(2,1)}, f32[64,512]{1,0:T(8,128)}, f32[64,512]{1,0:T(8,128)}, f32[64,512]{1,0:T...) custom-call(bf16[2,640,512]{2,1,0:T(8,128)(2,1)} %get-tuple-element.44.lo_in, ...), custom_call_target="tpu_custom_call" | custom-call | tf_op jit(solution)/shard_map/finish/pallas_call | solution.py:1001
  213.3 0.0 copy-done
  213.4 0.1 constant_dynamic-slice_fusion
  213.4 0.5 slice_bitcast_fusion.1
  214.0 0.6 dynamic_slice.11
  (4 shorter events, 0.0 us)
Async XLA Ops:
  209.3 4.0 %copy-start = (f32[16,512]{1,0:T(8,128)S(1)}, f32[16,512]{1,0:T(8,128)}, u32[]{:S(2)}) copy-start(f32[16,512]{1,0:T(8,128)} %get-tuple-element.66) | copy-start | bytes 98308
where the time goes:
time: 215 us
  Pallas kernels  210 us (98%)
  local copies, waits for them, and re-layouts  3.93 us (2%)
    pallas_call x1, Pallas kernels, last(): pl.pallas_call(functools.partial(last_kernel, F), out_shape=[jax.ShapeDty...  109 us
    pallas_call x1, Pallas kernels, first(): pl.pallas_call(functools.partial(first_kernel, F, n), out_shape=[jax.Shap...  97 us

commit v1 on v0

--- a/solution.py
+++ b/solution.py
@@ -236,7 +236,7 @@
         hook("mid", pr)
         lax.fori_loop(0, 2, lambda i, c: (tail_tile(i, False), c)[1], 0)
         hook("late", pr)
-        lax.fori_loop(2, 6, lambda i, c: (tail_tile(i, True), c)[1], 0)
+        lax.fori_loop(2, 6, lambda i, c: (hook("leaf", pr, i), tail_tile(i, True), c)[2], 0)
         first = pr * 384
 
         def put(i, x):
@@ -252,7 +252,7 @@
 
 
 class Dense:
-    def __init__(self, rows, width, oF_ref, dy_ref, woi_ref, wu_ref, rows_ref, dxl_ref, dx2_ref, g1_ref, vin_ref,
+    def __init__(self, rows, width, oF_ref, dy_ref, woi_ref, wu_ref, rows_ref, dxl_ref, dx2_ref, ga_ref, gb_ref, vin_ref,
                  a2s, gs, dus):
         self.__dict__.update({k: v for k, v in locals().items() if k != "self"})
         self.hidden = wu_ref.shape[0]
@@ -311,23 +311,23 @@
         add_sum(5, dyf)
 
     def gradients(self, F):
-        width, hidden, tiles, g1_ref = self.width, self.hidden, self.tiles, self.g1_ref
+        width, hidden, tiles, gb_ref = self.width, self.hidden, self.tiles, self.gb_ref
         r, ru = width // F, hidden // F
         nb = T // ru
         dy = self.dy_ref[...].reshape(2 * self.rows, width)
 
         def outer(t, c):
             val = mm_tn(self.gs[:, pl.ds(pl.multiple_of(t * T, T), T)], dy).astype(bf16)
-            g1_ref[pl.ds(t * nb, nb), 0:ru, :] = val.reshape(nb, ru, width)
+            self.ga_ref[pl.ds(t * nb, nb)] = val.reshape(nb, ru, width)
             return c
 
         lax.fori_loop(0, hidden // T, outer, 0)
         a2T = self.a2s[...].T
         for t in range(tiles):
             val = mm(a2T, self.dus[:, t * width:(t + 1) * width]).astype(bf16)
-            g1_ref[:, ru + t * r:ru + (t + 1) * r, :] = val.reshape(F, r, width)
+            gb_ref[:, t * r:(t + 1) * r, :] = val.reshape(F, r, width)
         val = mm(self.oF_ref[...], self.dxl_ref[...]).astype(bf16)
-        g1_ref[:, ru + tiles * r:ru + (tiles + 1) * r, :] = val.reshape(F, r, width)
+        gb_ref[:, tiles * r:(tiles + 1) * r, :] = val.reshape(F, r, width)
 
 
 def slope_parts(head, head_count, length):
@@ -369,9 +369,9 @@
 
 def first_kernel(F, n, parents_ref, tok_ref, cot_ref, wq_ref, wk_ref, wv_ref, wo_ref, wi_ref, wu_ref, vec_ref,
                  a1T_out, kaug_out, v_out, kT_out, qn_out, qT_out, oT_out, lse_out, wc_out, wo_out, xs_out, dxl_out,
-                 dx2_out, g1_out, lo_ref, vin_ref, rows_ref,
+                 dx2_out, ga_out, gb_out, y_out, vin_ref, rows_ref,
                  xt_ref, a1T_ref, kaug_ref, v_ref, kT_ref, qn_ref, qT_ref, oT_ref, lse_ref, oF_ref, dy_ref,
-                 wqkv_ref, woi_ref, wuf_ref, wc, dxl_ref, dx2_ref, g1_ref, a2s, gs, dus,
+                 wqkv_ref, woi_ref, wuf_ref, wc, dxl_ref, dx2_ref, ga_ref, gb_ref, a2s, gs, dus,
                  vecs, vT_scr, s_scr, tsend, trecv, gsend, grecv, osem):
     f, part, half, core, partner, sibling = where_am_i(F)
     rows, width = tok_ref.shape[1:]
@@ -535,7 +535,6 @@
             x_fwd.start()
             send_all(2)
             send_all(3)
-            dy_out.start()
 
         @pl.when(i == 3)
         def _():
@@ -555,12 +554,16 @@
             (oT_ref, oT_out), (lse_ref, lse_out),
             (woi_ref.at[pl.ds(pl.multiple_of(core * hw, hw), hw), 0:width], wo_out),
             (dxl_ref.at[0:rows], dxl_out.at[0]), (dxl_ref.at[rows:2 * rows], dxl_out.at[1]),
-            (dx2_ref.at[0:rows], dx2_out.at[0]), (dx2_ref.at[rows:2 * rows], dx2_out.at[1]), (g1_ref, g1_out)]
+            (dx2_ref.at[0:rows], dx2_out.at[0]), (dx2_ref.at[rows:2 * rows], dx2_out.at[1]), (ga_ref, ga_out), (gb_ref, gb_out)]
     copies = [pltpu.make_async_copy(a, b, osem.at[i]) for i, (a, b) in enumerate(outs)]
     for c in copies[:9]:
         c.start()
 
     def between(h):
+        @pl.when(h == 1)
+        def _():
+            dy_out.start()
+
         @pl.when(h == 2)
         def _():
             pass_on(2)
@@ -590,33 +593,28 @@
     dy_own.wait()
 
     vin_ref[...] = jnp.zeros_like(vin_ref)
-    dense = Dense(rows, width, oF_ref, dy_ref, woi_ref, wuf_ref, rows_ref, dxl_ref, dx2_ref, g1_ref, vin_ref,
+    dense = Dense(rows, width, oF_ref, dy_ref, woi_ref, wuf_ref, rows_ref, dxl_ref, dx2_ref, ga_ref, gb_ref, vin_ref,
                   a2s, gs, dus)
-    y_out = remote(xt_ref.at[other + 2 * (1 - half)], lo_ref.at[half],
-                   tsend.at[7], trecv.at[7], partner)
-    keep_y = pltpu.make_async_copy(xt_ref.at[other + 2 * half], lo_ref.at[half], osem.at[17])
+    keep_y = [pltpu.make_async_copy(xt_ref.at[other + 2 * i], y_out.at[i], osem.at[18 + i]) for i in range(2)]
 
     def dense_step(s, c):
         i = jnp.where(s == 0, half, 1 - half)
 
         @pl.when(s == 1)
         def _():
-            keep_y.start()
             dy_out.wait_recv()
 
         dense.chunk(i * rows, xt_ref[core + 2 * i], xt_ref.at[other + 2 * i])
         return c
 
     lax.fori_loop(0, 2, dense_step, 0)
-    y_out.start()
-    for c in copies[12:16]:
+    for c in keep_y + copies[12:16]:
         c.start()
     dense.gradients(F)
     copies[16].start()
-    for c in copies:
+    copies[17].start()
+    for c in copies + keep_y:
         c.wait()
-    keep_y.wait()
-    y_out.wait()
     dy_out.wait_send()
     x_out.wait_send()
     x_sib.wait_send()
@@ -638,17 +636,17 @@
     seg = rows // 5
     hidden = weights[4].shape[1]
     r, ru = width // F, hidden // F
-    R1 = ru + (hidden // width + 1) * r
+    R1 = (hidden // width + 1) * r
     two = 2 * rows
     keep = [((width, tree), bf16), ((20, seg, heads * 128), bf16), ((20, seg, hw), bf16), ((hw, tree), bf16),
             ((tree, hw), bf16), ((heads * 128, tree), bf16), ((hw, tree), bf16), ((heads * 8, tree), f32)]
     out = keep + [((width, 3 * hw), bf16), ((hw, width), bf16), ((2, rows, width), bf16), ((2, rows, width), bf16),
-                  ((2, rows, width), f32), ((F, R1, width), bf16), ((2, rows, width), bf16),
+                  ((2, rows, width), f32), ((F, ru, width), bf16), ((F, R1, width), bf16), ((2, rows, width), bf16),
                   ((16, width), f32), ((8, 6 * width + hidden), f32)]
     scratch = [((4, rows, width), bf16)] + keep + [
         ((2 * hw, two), bf16), ((2, rows, width), bf16), ((width, 3 * width), bf16), ((width, width + hidden), bf16),
         ((hidden, width), bf16), ((width, 3 * hw), bf16), ((two, width), bf16),
-        ((two, width), f32), ((F, R1, width), bf16), ((two, width), bf16), ((two, hidden), bf16),
+        ((two, width), f32), ((F, ru, width), bf16), ((F, R1, width), bf16), ((two, width), bf16), ((two, hidden), bf16),
         ((two, hidden), bf16), ((F,) + vec.shape, f32), ((heads * 80, tree), bf16), ((8 * seg, T), f32)]
     ANY = pl.BlockSpec(memory_space=pl.ANY)
     dma = pltpu.SemaphoreType.DMA
@@ -656,9 +654,9 @@
         functools.partial(first_kernel, F, n),
         out_shape=[jax.ShapeDtypeStruct(s, d) for s, d in out],
         in_specs=[SM, VM, ANY] + [VM] * 7,
-        out_specs=[ANY] * 15 + [VM] * 2,
+        out_specs=[ANY] * 16 + [VM] * 2,
         scratch_shapes=[pltpu.VMEM(s, d) for s, d in scratch] + [
-            dma((8,)), dma((8,)), dma((4, F)), dma((4, F)), dma((18,))],
+            dma((7,)), dma((7,)), dma((4, F)), dma((4, F)), dma((20,))],
         name="front",
         compiler_params=pltpu.CompilerParams(vmem_limit_bytes=64 << 20, collective_id=0, has_side_effects=True),
     )(parents, tokens, cotangent, *weights, vec)
@@ -740,13 +738,13 @@
             self._d(e).wait_send()
 
 
-def last_kernel(F, parents_ref, kaug_h, v_h, qT_h, kT_h, qn_h, oT_h, lse_h, a1T_h, wc_h, wo_h, xs_h, dxl_ref, dx2_h,
-                g1_ref, vin_ref, n1_ref,
-                gt_ref, gq_ref, fin1, vout_ref,
-                kaug_ref, v_ref, qT_ref, kT_ref, qn_ref, oT_ref, lse_ref, a1T_ref, wc, wo_scr, xs, dx2s,
+def last_kernel(F, parents_ref, kaug_h, v_h, qT_h, kT_h, qn_h, oT_h, lse_h, a1T_h, wc_h, wo_h, xs_h, dxl_ref, dx2_h, y_h,
+                ga_ref, gb_ref, vin_ref, n1_ref,
+                gt_ref, lo_ref, gq_ref, fina, finb, vout_ref,
+                kaug_ref, v_ref, qT_ref, kT_ref, qn_ref, oT_ref, lse_ref, a1T_ref, wc, wo_scr, xs, dx2s, ys,
                 dxs, doT, do, dqT, dqkv, accK, accV, das, dar,
-                a_sum, a_got, b_got, blk1, z1, sum2, got2, blk2, z2, fin2,
-                vs, vgot, dxo, tsend, trecv, send1, recv1, send2, recv2, vsend, vrecv, lsem):
+                suma, sumb, gota, gotb, planea, planeb, blka, blkb, za, zb, sum2, got2, blk2, z2, fin2,
+                vs, vgot, dxo, tsend, trecv, senda, recva, sendb, recvb, send2, recv2, vsend, vrecv, lsem):
     f, part, half, core, partner, sibling = where_am_i(F)
     planes = lax.axis_size("dp")
     plane = lax.axis_index("dp")
@@ -759,8 +757,8 @@
     seg = rows // 5
 
     pairs = [(wo_h, wo_scr), (qT_h, qT_ref), (kaug_h, kaug_ref), (v_h, v_ref), (kT_h, kT_ref), (qn_h, qn_ref),
-             (oT_h, oT_ref), (lse_h, lse_ref), (g1_ref.at[:, core], a_sum), (a1T_h, a1T_ref), (wc_h, wc), (xs_h, xs),
-             (dx2_h, dx2s)]
+             (oT_h, oT_ref), (lse_h, lse_ref), (ga_ref.at[:, core], suma), (gb_ref.at[:, core], sumb), (a1T_h, a1T_ref), (wc_h, wc), (xs_h, xs),
+             (dx2_h, dx2s), (y_h, ys)]
     loads = [pltpu.make_async_copy(a, b, lsem.at[i]) for i, (a, b) in enumerate(pairs)]
     for c in loads:
         c.start()
@@ -776,9 +774,13 @@
     pl.semaphore_wait(barrier, chips + planes - 1)
 
     dx_sw = remote(dxl_ref, dxs, tsend.at[0], trecv.at[0], sibling)
-    a_out = remote(g1_ref.at[:, other], a_got, tsend.at[1], trecv.at[1], sibling)
+    out_a = remote(ga_ref.at[:, other], gota, tsend.at[1], trecv.at[1], sibling)
+    out_b = remote(gb_ref.at[:, other], gotb, tsend.at[7], trecv.at[7], sibling)
+    y_out = remote(ys.at[1 - half], lo_ref.at[half], tsend.at[8], trecv.at[8], partner)
+    keep_y = pltpu.make_async_copy(ys.at[half], lo_ref.at[half], lsem.at[16])
     dx_sw.start()
-    a_out.start()
+    out_a.start()
+    out_b.start()
 
     def make_do(p, x):
         cols = pl.ds(pl.multiple_of(p * rows, rows), rows)
@@ -789,19 +791,24 @@
     loads[0].wait()
     lax.fori_loop(0, 2, lambda i, c: (make_do(core + 2 * i, dxl_ref[i]), c)[1], 0)
 
-    one = Chain(F, f, a_sum, b_got, blk1, z1, fin1, send1, recv1)
-    loads[8].wait()
-    a_out.wait_recv()
-
-    def add_block(j, c):
-        a_sum[j] = (fold(a_sum[j]) + fold(a_got[j])).astype(bf16)
-        return c
-
-    lax.fori_loop(0, chips, add_block, 0)
-    one.start_plane()
+    one_a = Chain(F, f, suma, planea, blka, za, fina, senda, recva)
+    one_b = Chain(F, f, sumb, planeb, blkb, zb, finb, sendb, recvb)
+
+    def add_sibling(load, arrived, mine, got):
+        load.wait()
+        arrived.wait_recv()
+
+        def add_block(j, c):
+            mine[j] = (fold(mine[j]) + fold(got[j])).astype(bf16)
+            return c
+
+        lax.fori_loop(0, chips, add_block, 0)
+
     dx_sw.wait_recv()
     lax.fori_loop(0, 2, lambda i, c: (make_do(other + 2 * i, dxs[i]), c)[1], 0)
-    for c in loads[1:8] + loads[9:]:
+    add_sibling(loads[8], out_a, suma, gota)
+    one_a.start_plane()
+    for c in loads[1:8]:
         c.wait()
 
     def chain(pr):
@@ -811,18 +818,42 @@
     r = width // F
     r2 = 2 * r
 
-    def hook(name, pr):
+    def hook(name, pr, i=None):
         if name == "mid":
+            @pl.when(pr == 0)
+            def _():
+                add_sibling(loads[9], out_b, sumb, gotb)
+                one_b.start_plane()
+
             @pl.when(pr == 1)
             def _():
-                one.start_z()
-                two[0].start_z()
+                one_b.start_z()
+                loads[14].wait()
+                y_out.start()
+                keep_y.start()
         if name == "late":
             @pl.when(pr == 1)
             def _():
-                one.start_back()
+                one_a.start_back()
+        if name == "leaf":
+            @pl.when((pr == 0) & (i == 5))
+            def _():
+                one_a.start_z()
+
+            @pl.when((pr == 1) & (i == 4))
+            def _():
+                one_b.start_back()
+                two[0].start_z()
+        if name == "end":
+            @pl.when(pr == 0)
+            def _():
+                for c in loads[10:14]:
+                    c.wait()
+
+            @pl.when(pr == 1)
+            def _():
                 two[0].start_back()
-        if name == "end":
+
             g = mm(a1T_ref[...], dqkv[:, :, pl.ds(pl.multiple_of(pr * 384, 384), 384)].reshape(tree, 384)).astype(bf16)
             for j in range(chips):
                 sum2[pr, j] = g[j * r2:(j + 1) * r2]
@@ -839,7 +870,7 @@
         return remote(das.at[i], dar.at[i], tsend.at[2 + s], trecv.at[2 + s], sibling)
 
     dx_out = remote(dxo.at[1 - half], gt_ref.at[half], tsend.at[4], trecv.at[4], partner)
-    keep_dx = pltpu.make_async_copy(dxo.at[half], gt_ref.at[half], lsem.at[13])
+    keep_dx = pltpu.make_async_copy(dxo.at[half], gt_ref.at[half], lsem.at[15])
     vs[0] = vin_ref[...]
     row = iota((16, width), 0)
 
@@ -904,7 +935,8 @@
     for e in range(1, planes):
         v_z(e, plane).start()
 
-    one.receive()
+    one_a.receive()
+    one_b.receive()
     s_out = []
     for pr in range(2):
         two[pr].receive()
@@ -923,16 +955,19 @@
         c.wait()
     dx_out.wait()
     keep_dx.wait()
-    one.close()
+    keep_y.wait()
+    y_out.wait()
+    one_a.close()
+    one_b.close()
     for c in two:
         c.close()
-    for c in [dx_sw, a_out, v_sib, da_out(0), da_out(1)] + v_chip:
+    for c in [dx_sw, out_a, out_b, v_sib, da_out(0), da_out(1)] + v_chip:
         c.wait_send()
     for e in range(1, planes):
         v_z(e, plane).wait_send()
 
 
-def last(F, DP, parents, kept, wc, wo, xs, dxl, dx2, g1, vin, rows_vec):
+def last(F, DP, parents, kept, wc, wo, xs, dxl, dx2, y, ga, gb, vin, rows_vec):
     a1T, kaug, v, kT, qn, qT, oT, lse = kept
     _, rows, width = dxl.shape
     heads = H // 2
@@ -941,24 +976,26 @@
     seg = rows // 5
     chips = F // 2
     r = width // F
-    R1 = g1.shape[2]
+    RA, RB = ga.shape[2], gb.shape[2]
     r2 = 2 * r
 
     def zrows(n):
         return -(-n // (16 * DP)) * 16
 
-    Z1, Z2 = zrows(R1), zrows(r2)
+    ZA, ZB, Z2 = zrows(RA), zrows(RB), zrows(r2)
     ANY = pl.BlockSpec(memory_space=pl.ANY)
     dma = pltpu.SemaphoreType.DMA
-    out = [((2, rows, width), bf16), ((2, 2, r, 384), bf16), ((Z1 * DP, width), bf16), ((16, width), f32)]
+    out = [((2, rows, width), bf16), ((2, rows, width), bf16), ((2, 2, r, 384), bf16), ((ZA * DP, width), bf16),
+           ((ZB * DP, width), bf16), ((16, width), f32)]
     big = [kaug, v, qT, kT, qn, oT, lse, a1T, wc, wo, xs]
     scratch = [(a.shape, a.dtype) for a in big] + [
-        ((2, rows, width), f32),
+        ((2, rows, width), f32), ((2, rows, width), bf16),
         ((2, rows, width), bf16), ((hw, tree), bf16), ((tree, hw), bf16), ((128, tree), bf16),
         ((20, seg, 3 * hw), bf16), ((20, seg, 128), f32), ((20, seg, 128), f32),
         ((2, rows, width), bf16), ((2, rows, width), bf16),
-        ((chips, R1, width), bf16), ((chips, R1, width), bf16), ((chips - 1, R1, width), bf16),
-        ((Z1 * DP, width), bf16), ((DP - 1, Z1, width), bf16),
+        ((chips, RA, width), bf16), ((chips, RB, width), bf16), ((chips, RA, width), bf16), ((chips, RB, width), bf16),
+        ((chips - 1, RA, width), bf16), ((chips - 1, RB, width), bf16), ((ZA * DP, width), bf16),
+        ((ZB * DP, width), bf16), ((DP - 1, ZA, width), bf16), ((DP - 1, ZB, width), bf16),
         ((2, chips, r2, 384), bf16), ((2, chips - 1, r2, 384), bf16), ((2, Z2 * DP, 384), bf16),
         ((2, DP - 1, Z2, 384), bf16), ((2, Z2 * DP, 384), bf16),
         ((2, 16, width), f32), ((chips + DP, 16, width), f32), ((2, rows, width), bf16),
@@ -967,26 +1004,26 @@
     return pl.pallas_call(
         functools.partial(last_kernel, F),
         out_shape=[jax.ShapeDtypeStruct(s, d) for s, d in out],
-        in_specs=[SM] + [ANY] * 11 + [VM, ANY, ANY, VM, VM],
-        out_specs=[ANY] + [VM] * 3,
+        in_specs=[SM] + [ANY] * 11 + [VM, ANY, ANY, ANY, ANY, VM, VM],
+        out_specs=[ANY, ANY] + [VM] * 4,
         scratch_shapes=[pltpu.VMEM(s, d) for s, d in scratch] + [
-            dma((7,)), dma((7,)), dma((nsem,)), dma((nsem,)), dma((2, nsem)), dma((2, nsem)),
-            dma((chips + DP,)), dma((chips + DP,)), dma((14,))],
+            dma((9,)), dma((9,)), dma((nsem,)), dma((nsem,)), dma((nsem,)), dma((nsem,)), dma((2, nsem)), dma((2, nsem)),
+            dma((chips + DP,)), dma((chips + DP,)), dma((17,))],
         name="back",
         compiler_params=pltpu.CompilerParams(vmem_limit_bytes=64 << 20, collective_id=1, has_side_effects=True),
-    )(parents, *big, dxl, dx2, g1, vin, rows_vec)
-
-
-def finish_kernel(lo_in, gt_in, fin1, gq, lo_ref, gt_ref, gwq_ref, gwk_ref, gwv_ref, gwo_ref, gwi_ref, gwu_ref):
+    )(parents, *big, dxl, dx2, y, ga, gb, vin, rows_vec)
+
+
+def finish_kernel(lo_in, gt_in, fina, finb, gq, lo_ref, gt_ref, gwq_ref, gwk_ref, gwv_ref, gwo_ref, gwi_ref, gwu_ref):
     lo_ref[...] = lo_in[...]
     gt_ref[...] = gt_in[...]
     r, width = gwo_ref.shape
     ru = gwu_ref.shape[0]
-    gwu_ref[...] = fold(fin1[0:ru])
+    gwu_ref[...] = fold(fina[0:ru])
     pieces = gwi_ref.shape[1] // width
     for c in range(pieces):
-        gwi_ref[:, c * width:(c + 1) * width] = fold(fin1[ru + c * r:ru + (c + 1) * r])
-    gwo_ref[...] = fold(fin1[ru + pieces * r:ru + (pieces + 1) * r])
+        gwi_ref[:, c * width:(c + 1) * width] = fold(finb[c * r:(c + 1) * r])
+    gwo_ref[...] = fold(finb[pieces * r:(pieces + 1) * r])
     for k, ref in enumerate((gwq_ref, gwk_ref, gwv_ref)):
         for c in range(2):
             for pr in range(2):
@@ -994,7 +1031,7 @@
                 ref[:, at:at + 128] = fold(gq[c, pr, :, 128 * k:128 * k + 128])
 
 
-def finish(F, lo, gt, fin1, gq, hidden):
+def finish(F, lo, gt, fina, finb, gq, hidden):
     width = lo.shape[2]
     r, ru = width // F, hidden // F
     shapes = [(r, width)] * 4 + [(r, hidden), (ru, width)]
@@ -1002,10 +1039,10 @@
         finish_kernel,
         out_shape=[jax.ShapeDtypeStruct(lo.shape, bf16), jax.ShapeDtypeStruct(gt.shape, bf16)]
         + [jax.ShapeDtypeStruct(s, f32) for s in shapes],
-        in_specs=[VM] * 4,
+        in_specs=[VM] * 5,
         out_specs=[VM] * 8,
         name="finish",
-    )(lo, gt, fin1, gq)
+    )(lo, gt, fina, finb, gq)
 
 
 def on_device(tokens, parents, n1g, n1b, wq, wk, wv, wo, ob, n2g, n2b, wi, ib, wu, ub, cotangent):
@@ -1023,12 +1060,12 @@
     vec = jnp.broadcast_to(jnp.pad(vec, (0, -vec.shape[0] % 128)), (8, vec.shape[0] + -vec.shape[0] % 128))
     hidden = wi.shape[1]
     ru = hidden // F
-    (a1T, kaug, v, kT, qn, qT, oT, lse, wc, wo_own, xs, dxl, dx2, g1, lo, vin, vrows) = first(
+    (a1T, kaug, v, kT, qn, qT, oT, lse, wc, wo_own, xs, dxl, dx2, ga, gb, y, vin, vrows) = first(
         F, parent_row, tokens[0], cotangent[0], (wq, wk, wv, wo, wi, wu), vec, n)
-    gt, gq, fin1, vout = last(
-        F, lax.axis_size("dp"), parent_row, (a1T, kaug, v, kT, qn, qT, oT, lse), wc, wo_own, xs, dxl, dx2,
-        g1.reshape(F // 2, 2, -1, width), vin, vrows)
-    lo, gt, gwq, gwk, gwv, gwo, gwi, gwu = finish(F, lo, gt, fin1, gq, hidden)
+    gt, lo, gq, fina, finb, vout = last(
+        F, lax.axis_size("dp"), parent_row, (a1T, kaug, v, kT, qn, qT, oT, lse), wc, wo_own, xs, dxl, dx2, y,
+        ga.reshape(F // 2, 2, -1, width), gb.reshape(F // 2, 2, -1, width), vin, vrows)
+    lo, gt, gwq, gwk, gwv, gwo, gwi, gwu = finish(F, lo, gt, fina, finb, gq, hidden)
     sv = lax.dynamic_slice_in_dim(vout[:6], fi * n, n, 1)
     sib = lax.dynamic_slice_in_dim(vout[6:6 + hidden // width].reshape(-1), fi * ru, ru, 0)
     return (lo[None], gt[None], sv[0], sv[1], gwq, gwk, gwv, gwo, sv[2], sv[3], sv[4], gwi, sib, gwu, sv[5])

time: 215 us -> 197 us (0.916)
  Pallas kernels: 210 us -> 192 us
    pallas_call x1, Pallas kernels: 109 us -> 97.1 us  [last(): pl.pallas_call(functools.partial(last_kernel, F), out_shape=[jax.ShapeDty...]
    pallas_call x1, Pallas kernels: 97 us -> 91.4 us  [first(): pl.pallas_call(functools.partial(first_kernel, F, n), out_shape=[jax.Shap...]
where the time goes in v1:
time: 197 us
  Pallas kernels  192 us (97%)
  local copies, waits for them, and re-layouts  3.93 us (2%)
    pallas_call x1, Pallas kernels, last(): pl.pallas_call(functools.partial(last_kernel, F), out_shape=[jax.ShapeDty...  97.1 us
    pallas_call x1, Pallas kernels, first(): pl.pallas_call(functools.partial(first_kernel, F, n), out_shape=[jax.Shap...  91.4 us
    pallas_call x1, Pallas kernels, finish(): pl.pallas_call(finish_kernel, out_shape=[jax.ShapeDtypeStruct(lo.shape, b...  3.98 us

profile of v1, /device:TPU:0, one launch (start us, length us, event | category | flops | bytes accessed | tf_op | source)
XLA Modules:
  0.0 197.2 jit_solution(15167926235421776693)
XLA Ops:
  0.7 1.2 dynamic-slice_bitcast_fusion.parents_ref
  1.9 0.8 concatenate.3
  2.8 0.6 broadcast_in_dim.9.vec_ref
  3.4 91.4 %front.1 = (bf16[512,2560]{1,0:T(8,128)(2,1)}, bf16[20,128,512]{2,1,0:T(8,128)(2,1)}, bf16[20,128,256]{2,1,0:T(8,128)(2,1)}, bf16[256,2560]{1,0:T(8,128)(2,1)}, ...) custom-call(s32[16]{0:T(128)} %dynamic-slice_bitcast_fusion.parents_, ...), custom_call_target="tpu_custom_call" | custom-call | tf_op jit(solution)/shard_map/front/pallas_call | solution.py:653
  94.8 97.1 %back.1 = (bf16[2,640,512]{2,1,0:T(8,128)(2,1)}, bf16[2,640,512]{2,1,0:T(8,128)(2,1)}, bf16[2,2,64,384]{3,2,1,0:T(8,128)(2,1)}, bf16[256,512]{1,0:T(8,128)(2,1)}...) custom-call(s32[16]{0:T(128)} %dynamic-slice_bitcast_fusion.parents_ref, bf16[20,128,512]{2,1,0:T(8,128)(2,1)} %get-tuple-element.47.kaug_h, ...), custom_call_target="tpu_custom_call" | custom-call | tf_op jit(solution)/shard_map/back/pallas_call | solution.py:1004
  191.9 0.0 copy-start
  191.9 4.0 %finish.1 = (bf16[2,640,512]{2,1,0:T(8,128)(2,1)}, bf16[2,640,512]{2,1,0:T(8,128)(2,1)}, f32[64,512]{1,0:T(8,128)}, f32[64,512]{1,0:T(8,128)}, f32[64,512]{1,0:T...) custom-call(bf16[2,640,512]{2,1,0:T(8,128)(2,1)} %get-tuple-element.65.lo_in, ...), custom_call_target="tpu_custom_call" | custom-call | tf_op jit(solution)/shard_map/finish/pallas_call | solution.py:1038
  195.9 0.0 copy-done
  195.9 0.1 constant_dynamic-slice_fusion
  196.0 0.5 slice_bitcast_fusion.1
  196.5 0.6 dynamic_slice.11
  (4 shorter events, 0.0 us)
Async XLA Ops:
  191.9 4.0 %copy-start = (f32[16,512]{1,0:T(8,128)S(1)}, f32[16,512]{1,0:T(8,128)}, u32[]{:S(2)}) copy-start(f32[16,512]{1,0:T(8,128)} %get-tuple-element.72) | copy-start | bytes 98308

commit v2 on v1

--- a/solution.py
+++ b/solution.py
@@ -40,95 +40,105 @@
     return out
 
 
-def attend(heads, seg, parents_ref, kaug_ref, qT_ref, vT_ref, oT_ref, lse_ref, s_scr, between):
-    trunk = 8 * seg
-    ntr = trunk // T
+def attend(heads, seg, parents_ref, kaug_ref, qT_ref, vT_ref, oT_ref, lse_ref, s_refs, hook):
+    ntr = 8 * seg // T
     vr = vT_ref.shape[0] // heads
     causal_t = iota((T, T), 0) <= iota((T, T), 1)
     causal_b = iota((seg, seg), 0) <= iota((seg, seg), 1)
-
-    def finish(h, cols, m, acc):
-        l = acc[64:65, :]
-        oT_ref[pl.ds(pl.multiple_of(h * 64, 64), 64), cols] = (acc[:64] / l).astype(bf16)
-        lse_ref[pl.ds(pl.multiple_of(h * 8, 8), 8), cols] = jnp.broadcast_to(m + jnp.log(l), (8, T))
-
-    def head(h, _):
-        between(h)
-        hk = pl.ds(pl.multiple_of(h * 128, 128), 128)
-        hv = pl.ds(pl.multiple_of(h * vr, vr), vr)
-
-        def keys(blk, n):
-            return kaug_ref[pl.ds(blk, n), :, hk].reshape(n * seg, 128)
-
-        def full_scores(q, n):
+    G = heads
+
+    def group(g, _):
+        hook(0)
+        hs = [g * G + e for e in range(G)]
+        hk = [pl.ds(pl.multiple_of(h * 128, 128), 128) for h in hs]
+        hv = [pl.ds(pl.multiple_of(h * vr, vr), vr) for h in hs]
+
+        def keys(e, blk, n):
+            return kaug_ref[pl.ds(blk, n), :, hk[e]].reshape(n * seg, 128)
+
+        def finish(e, cols, m, acc):
+            h = hs[e]
+            l = acc[64:65, :]
+            oT_ref[pl.ds(pl.multiple_of(h * 64, 64), 64), cols] = (acc[:64] / l).astype(bf16)
+            lse_ref[pl.ds(pl.multiple_of(h * 8, 8), 8), cols] = jnp.broadcast_to(m + jnp.log(l), (8, T))
+
+        def full_scores(e, q, n):
             m = None
             for c in range(n):
-                s = mm(keys(2 * c, 2), q)
-                s_scr[c * T:(c + 1) * T, :] = s
+                s = mm(keys(e, 2 * c, 2), q)
+                s_refs[e][c * T:(c + 1) * T, :] = s
                 cm = jnp.max(s, axis=0, keepdims=True)
                 m = cm if m is None else jnp.maximum(m, cm)
             return m
 
-        def full_mix(m, n, acc):
+        def full_mix(e, m, n, acc):
             for c in range(n):
-                p = jnp.exp(s_scr[c * T:(c + 1) * T, :] - m).astype(bf16)
-                t = mm(vT_ref[hv, c * T:(c + 1) * T], p)
+                p = jnp.exp(s_refs[e][c * T:(c + 1) * T, :] - m).astype(bf16)
+                t = mm(vT_ref[hv[e], c * T:(c + 1) * T], p)
                 acc = t if acc is None else acc + t
             return acc
 
         for t in range(ntr):
             cols = slice(t * T, (t + 1) * T)
-            q = qT_ref[hk, cols]
-            sd = jnp.where(causal_t, mm(keys(2 * t, 2), q), -1e30)
-            m = jnp.max(sd, axis=0, keepdims=True)
-            if t:
-                m = jnp.maximum(m, full_scores(q, t))
-            acc = mm(vT_ref[hv, cols], jnp.exp(sd - m).astype(bf16))
-            acc = full_mix(m, t, acc)
-            finish(h, cols, m, acc)
+            sds, ms = [], []
+            for e in range(G):
+                q = qT_ref[hk[e], cols]
+                sd = jnp.where(causal_t, mm(keys(e, 2 * t, 2), q), -1e30)
+                m = jnp.max(sd, axis=0, keepdims=True)
+                if t:
+                    m = jnp.maximum(m, full_scores(e, q, t))
+                sds.append(sd)
+                ms.append(m)
+            for e in range(G):
+                acc = mm(vT_ref[hv[e], cols], jnp.exp(sds[e] - ms[e]).astype(bf16))
+                acc = full_mix(e, ms[e], t, acc)
+                finish(e, cols, ms[e], acc)
 
         def tail_tile(i, leaf):
             b0 = 8 + 2 * i
             cols = pl.ds(pl.multiple_of(b0 * seg, T), T)
-            q = qT_ref[hk, cols]
-            rows = []
-            for half in range(2):
-                rows.append([b0 + half])
-                if leaf:
-                    rows[-1].append(parents_ref[b0 + half - 7])
-            m = full_scores(q, ntr)
-            ext = []
-            for e in range(len(rows[0])):
-                pieces = []
-                for half in range(2):
-                    kk = keys(rows[half][0], 1) if e == 0 else chosen(rows[half][1], lambda b: keys(8 + b, 1))
-                    s = mm(kk, q[:, half * seg:(half + 1) * seg])
-                    if e == 0:
-                        s = jnp.where(causal_b, s, -1e30)
-                    pieces.append(s)
-                s = jnp.concatenate(pieces, axis=1)
-                m = jnp.maximum(m, jnp.max(s, axis=0, keepdims=True))
-                ext.append(s)
-            acc = None
-            for e in range(len(ext)):
-                p = jnp.exp(ext[e] - m).astype(bf16)
-                t = []
-                for half in range(2):
-                    if e == 0:
-                        vv = vT_ref[hv, pl.ds(pl.multiple_of(rows[half][0] * seg, seg), seg)]
-                    else:
-                        vv = chosen(rows[half][1], lambda b: vT_ref[hv, (8 + b) * seg:(9 + b) * seg])
-                    t.append(mm(vv, p[:, half * seg:(half + 1) * seg]))
-                t = jnp.concatenate(t, axis=1)
-                acc = t if acc is None else acc + t
-            acc = full_mix(m, ntr, acc)
-            finish(h, cols, m, acc)
-
+            pars = [parents_ref[b0 + half - 7] for half in range(2)] if leaf else None
+            exts, ms = [], []
+            for e in range(G):
+                q = qT_ref[hk[e], cols]
+                m = full_scores(e, q, ntr)
+                ext = []
+                for x in range(2 if leaf else 1):
+                    pieces = []
+                    for half in range(2):
+                        kk = keys(e, b0 + half, 1) if x == 0 else chosen(pars[half], lambda b: keys(e, 8 + b, 1))
+                        s = mm(kk, q[:, half * seg:(half + 1) * seg])
+                        if x == 0:
+                            s = jnp.where(causal_b, s, -1e30)
+                        pieces.append(s)
+                    s = jnp.concatenate(pieces, axis=1)
+                    m = jnp.maximum(m, jnp.max(s, axis=0, keepdims=True))
+                    ext.append(s)
+                exts.append(ext)
+                ms.append(m)
+            for e in range(G):
+                acc = None
+                for x, s in enumerate(exts[e]):
+                    p = jnp.exp(s - ms[e]).astype(bf16)
+                    t = []
+                    for half in range(2):
+                        if x == 0:
+                            vv = vT_ref[hv[e], pl.ds(pl.multiple_of((b0 + half) * seg, seg), seg)]
+                        else:
+                            vv = chosen(pars[half], lambda b: vT_ref[hv[e], (8 + b) * seg:(9 + b) * seg])
+                        t.append(mm(vv, p[:, half * seg:(half + 1) * seg]))
+                    t = jnp.concatenate(t, axis=1)
+                    acc = t if acc is None else acc + t
+                acc = full_mix(e, ms[e], ntr, acc)
+                finish(e, cols, ms[e], acc)
+
+        hook(1)
         lax.fori_loop(0, 2, lambda i, c: (tail_tile(i, False), c)[1], 0)
-        lax.fori_loop(2, 6, lambda i, c: (tail_tile(i, True), c)[1], 0)
+        hook(2)
+        lax.fori_loop(2, 6, lambda i, c: (hook(3, i), tail_tile(i, True), c)[2], 0)
         return 0
 
-    lax.fori_loop(0, heads, head, 0)
+    lax.fori_loop(0, heads // G, group, 0)
 
 
 def attend_back(heads, seg, parents_ref, kaug_ref, v_ref, qT_ref, doT_ref, kT_ref, do_ref, qn_ref,
@@ -164,9 +174,8 @@
                 delta.append(jnp.sum(prod[64 * e:64 * e + 64], axis=0, keepdims=True))
             return q, do, lse, delta, stack(do_ref[cols, lanes]), stack(qn_ref[cols, lanes])
 
-        def piece(blk, n, sl, args, mask, par=None):
+        def front(blk, n, sl, args, mask, par=None):
             q, do, lse, delta, rv, rk = args
-            ps, dss, dq = [], [], []
 
             def rows_of(ref, at):
                 if par is None:
@@ -174,20 +183,25 @@
                 return chosen(par, lambda b: ref[8 + b, :, at])
 
             vv = rows_of(v_ref, lanes)
+            s = [mm(rows_of(kaug_ref, hk[e]), q[e][:, sl]) for e in range(2)]
+            dp = [mm(vv, do[e][:, sl]) for e in range(2)]
+            return s, dp
+
+        def rear(blk, n, sl, args, mask, par, s, dp):
+            q, do, lse, delta, rv, rk = args
+            ps, dss, dq = [], [], []
             for e in range(2):
-                kk = rows_of(kaug_ref, hk[e])
-                p = jnp.exp(mm(kk, q[e][:, sl]) - lse[e][:, sl])
+                p = jnp.exp(s[e] - lse[e][:, sl])
                 if mask is not None:
                     p = jnp.where(mask, p, 0.0)
-                dp = mm(vv, do[e][:, sl])
-                ds = (p * (dp - delta[e][:, sl])).astype(bf16)
+                dss.append((p * (dp[e] - delta[e][:, sl])).astype(bf16))
+                ps.append(p.astype(bf16))
+            for e in range(2):
                 if par is None:
                     kT = kT_ref[h64[e], pl.ds(pl.multiple_of(blk * seg, seg), n * seg)]
                 else:
                     kT = chosen(par, lambda b: kT_ref[h64[e], (8 + b) * seg:(9 + b) * seg])
-                dq.append(mm(kT, ds))
-                ps.append(p.astype(bf16))
-                dss.append(ds)
+                dq.append(mm(kT, dss[e]))
             if sl.stop - sl.start != T:
                 rv = jnp.concatenate([rv[sl], rv[T + sl.start:T + sl.stop]], axis=0)
                 rk = jnp.concatenate([rk[sl], rk[T + sl.start:T + sl.stop]], axis=0)
@@ -203,6 +217,18 @@
                     accV[8 + b] += av * here
             return dq
 
+        def run(items):
+            out = []
+            ready = []
+            for item in items:
+                ready.append((item, front(*item)))
+                if len(ready) > 2:
+                    it, (s, dp) = ready.pop(0)
+                    out.append(rear(*it, s, dp))
+            for it, (s, dp) in ready:
+                out.append(rear(*it, s, dp))
+            return out
+
         def emit(cols, dq):
             for e in range(2):
                 dqT_ref[64 * e:64 * e + 64, cols] = (dq[e] * 0.125).astype(bf16)
@@ -211,26 +237,27 @@
         for t in range(ntr):
             cols = slice(t * T, (t + 1) * T)
             args = prep(cols)
-            dq = piece(2 * t, 2, full, args, causal_t)
-            for c in range(t):
-                dq = [a + b for a, b in zip(dq, piece(2 * c, 2, full, args, None))]
-            emit(cols, dq)
+            items = [(2 * t, 2, full, args, causal_t, None)] + [(2 * c, 2, full, args, None, None) for c in range(t)]
+            res = run(items)
+            emit(cols, [sum(x[e] for x in res) for e in range(2)])
 
         def tail_tile(i, leaf):
             b0 = 8 + 2 * i
             cols = pl.ds(pl.multiple_of(b0 * seg, T), T)
             args = prep(cols)
-            halves = []
+            items = []
             for half in range(2):
                 sl = slice(half * seg, (half + 1) * seg)
-                d = piece(b0 + half, 1, sl, args, causal_b)
+                items.append((b0 + half, 1, sl, args, causal_b, None))
                 if leaf:
-                    par = parents_ref[b0 + half - 7]
-                    d = [x + y for x, y in zip(d, piece(8, 1, sl, args, None, par))]
-                halves.append(d)
-            dq = [jnp.concatenate([halves[0][e], halves[1][e]], axis=1) for e in range(2)]
-            for c in range(ntr):
-                dq = [a + b for a, b in zip(dq, piece(2 * c, 2, full, args, None))]
+                    items.append((8, 1, sl, args, None, parents_ref[b0 + half - 7]))
+            k = len(items) // 2
+            items += [(2 * c, 2, full, args, None, None) for c in range(ntr)]
+            res = run(items)
+            dq = []
+            for e in range(2):
+                halves = [sum(x[e] for x in res[h * k:(h + 1) * k]) for h in range(2)]
+                dq.append(jnp.concatenate(halves, axis=1) + sum(x[e] for x in res[2 * k:]))
             emit(cols, dq)
 
         hook("mid", pr)
@@ -438,14 +465,15 @@
     x_sib = remote(tok_ref.at[half], xt_ref.at[part], tsend.at[1], trecv.at[1], sibling)
     x_fwd = remote(xt_ref.at[part2], xt_ref.at[part2], tsend.at[2], trecv.at[2], sibling)
     dy_out = remote(cot_ref.at[1 - half], dy_ref.at[half], tsend.at[3], trecv.at[3], partner)
+    x_own = pltpu.make_async_copy(tok_ref.at[half], xt_ref.at[part], osem.at[20])
     dy_own = pltpu.make_async_copy(cot_ref.at[half], dy_ref.at[half], tsend.at[4])
 
     send_all(0)
     send_all(1)
     x_out.start()
     x_sib.start()
+    x_own.start()
     dy_own.start()
-    xt_ref[part] = tok_ref[half]
     woi_ref[own, 0:width] = wo_ref[...].astype(bf16)
     woi_ref[own, width:] = wi_ref[...].astype(bf16)
     wuf_ref[ownu, :] = wu_ref[...].astype(bf16)
@@ -524,6 +552,7 @@
                 kk = k[b * seg:(b + 1) * seg, 128 * (h // 2):128 * (h // 2) + 128]
                 kaug_ref[blk, :, 128 * h:128 * h + 128] = jnp.where(keep, kk, aug)
 
+    x_own.wait()
     x_sib.wait_recv()
 
     def visit(i, c):
@@ -559,16 +588,17 @@
     for c in copies[:9]:
         c.start()
 
-    def between(h):
-        @pl.when(h == 1)
-        def _():
+    s_refs = [dx2_ref.at[0:8 * seg, 0:T], dx2_ref.at[0:8 * seg, T:2 * T], s_scr.at[0], s_scr.at[1]]
+
+    def hook(stage, i=None):
+        if stage == 1:
             dy_out.start()
-
-        @pl.when(h == 2)
-        def _():
-            pass_on(2)
-
-    attend(heads, seg, parents_ref, kaug_ref, qT_ref, vT_scr, oT_ref, lse_ref, s_scr, between)
+        if stage == 3:
+            @pl.when(i == 4)
+            def _():
+                pass_on(2)
+
+    attend(heads, seg, parents_ref, kaug_ref, qT_ref, vT_scr, oT_ref, lse_ref, s_refs, hook)
 
     other = 1 - core
     sent = []
@@ -647,16 +677,16 @@
         ((2 * hw, two), bf16), ((2, rows, width), bf16), ((width, 3 * width), bf16), ((width, width + hidden), bf16),
         ((hidden, width), bf16), ((width, 3 * hw), bf16), ((two, width), bf16),
         ((two, width), f32), ((F, ru, width), bf16), ((F, R1, width), bf16), ((two, width), bf16), ((two, hidden), bf16),
-        ((two, hidden), bf16), ((F,) + vec.shape, f32), ((heads * 80, tree), bf16), ((8 * seg, T), f32)]
+        ((two, hidden), bf16), ((F,) + vec.shape, f32), ((heads * 80, tree), bf16), ((2, 8 * seg, T), f32)]
     ANY = pl.BlockSpec(memory_space=pl.ANY)
     dma = pltpu.SemaphoreType.DMA
     return pl.pallas_call(
         functools.partial(first_kernel, F, n),
         out_shape=[jax.ShapeDtypeStruct(s, d) for s, d in out],
-        in_specs=[SM, VM, ANY] + [VM] * 7,
+        in_specs=[SM, ANY, ANY] + [VM] * 7,
         out_specs=[ANY] * 16 + [VM] * 2,
         scratch_shapes=[pltpu.VMEM(s, d) for s, d in scratch] + [
-            dma((7,)), dma((7,)), dma((4, F)), dma((4, F)), dma((20,))],
+            dma((7,)), dma((7,)), dma((4, F)), dma((4, F)), dma((21,))],
         name="front",
         compiler_params=pltpu.CompilerParams(vmem_limit_bytes=64 << 20, collective_id=0, has_side_effects=True),
     )(parents, tokens, cotangent, *weights, vec)
@@ -667,7 +697,8 @@
 
 
 class Chain:
-    def __init__(self, F, f, sums, got, block, zgot, final, send, recv):
+    def __init__(self, F, f, sums, got, block, zgot, final, send, recv, stages=2):
+        self.square = F == 8 and stages == 2
         self.F, self.f, self.sums, self.got, self.block = F, f, sums, got, block
         self.zgot, self.final, self.send, self.recv = zgot, final, send, recv
         self.chip = f // 2
@@ -681,6 +712,18 @@
         return remote(self.sums.at[lax.rem(self.chip + d, self.chips)], self.got.at[d - 1],
                       self.send.at[d], self.recv.at[d], lax.rem(self.f + 2 * d, self.F))
 
+    def _square(self):
+        core = lax.rem(self.f, 2)
+        x, y = lax.rem(self.chip, 2), self.chip // 2
+        along_x, along_y = 2 * y + 1 - x, 2 * (1 - y) + x
+        first = jnp.where(core == 0, along_x, along_y)
+        second = jnp.where(core == 0, along_y, along_x)
+        last = 2 * (1 - y) + 1 - x
+        one = [remote(self.sums.at[first], self.got.at[0], self.send.at[1], self.recv.at[1], 2 * first + core),
+               remote(self.sums.at[last], self.got.at[1], self.send.at[2], self.recv.at[2], 2 * first + core)]
+        two = remote(self.sums.at[second], self.got.at[2], self.send.at[3], self.recv.at[3], 2 * second + core)
+        return one, two, second
+
     def _chunk(self, z):
         return pl.ds(pl.multiple_of(z * self.zrows, 16), self.zrows)
 
@@ -702,15 +745,31 @@
             device_id={"dp": z}, device_id_type=pl.DeviceIdType.MESH)
 
     def start_plane(self):
+        if self.square:
+            for c in self._square()[0]:
+                c.start()
+            return
         for d in range(1, self.chips):
             self._b(d).start()
 
+    def mid_plane(self):
+        if self.square:
+            one, two, second = self._square()
+            for c in one:
+                c.wait_recv()
+            self.sums[second] = (fold(self.sums[second]) + fold(self.got[1])).astype(bf16)
+            two.start()
+
     def start_z(self):
-        for d in range(1, self.chips):
-            self._b(d).wait_recv()
-        total = fold(self.sums[self.chip])
-        for d in range(1, self.chips):
-            total = total + fold(self.got[d - 1])
+        if self.square:
+            self._square()[1].wait_recv()
+            total = fold(self.sums[self.chip]) + fold(self.got[0]) + fold(self.got[2])
+        else:
+            for d in range(1, self.chips):
+                self._b(d).wait_recv()
+            total = fold(self.sums[self.chip])
+            for d in range(1, self.chips):
+                total = total + fold(self.got[d - 1])
         self.block[0:self.rows] = total.astype(bf16)
         for e in range(1, self.planes):
             self._c(e).start()
@@ -731,8 +790,13 @@
             self._d(e, lax.rem(self.plane + self.planes - e, self.planes)).wait_recv()
 
     def close(self):
-        for d in range(1, self.chips):
-            self._b(d).wait_send()
+        if self.square:
+            one, two, _ = self._square()
+            for c in one + [two]:
+                c.wait_send()
+        else:
+            for d in range(1, self.chips):
+                self._b(d).wait_send()
         for e in range(1, self.planes):
             self._c(e).wait_send()
             self._d(e).wait_send()
@@ -812,7 +876,7 @@
         c.wait()
 
     def chain(pr):
-        return Chain(F, f, sum2.at[pr], got2.at[pr], blk2.at[pr], z2.at[pr], fin2.at[pr], send2.at[pr], recv2.at[pr])
+        return Chain(F, f, sum2.at[pr], got2.at[pr], blk2.at[pr], z2.at[pr], fin2.at[pr], send2.at[pr], recv2.at[pr], 1)
 
     two = [chain(0), chain(1)]
     r = width // F
@@ -832,6 +896,10 @@
                 y_out.start()
                 keep_y.start()
         if name == "late":
+            @pl.when(pr == 0)
+            def _():
+                one_a.mid_plane()
+
             @pl.when(pr == 1)
             def _():
                 one_a.start_back()
@@ -839,6 +907,7 @@
             @pl.when((pr == 0) & (i == 5))
             def _():
                 one_a.start_z()
+                one_b.mid_plane()
 
             @pl.when((pr == 1) & (i == 4))
             def _():
@@ -914,17 +983,7 @@
     v_sib.start()
     two[1].start_z()
     v_sib.wait_recv()
-    vs[1] = vs[0] + vgot[0]
-    v_chip = [remote(vs.at[1], vgot.at[d], vsend.at[d], vrecv.at[d], lax.rem(f + 2 * d, F)) for d in range(1, chips)]
-    for c in v_chip:
-        c.start()
-    two[1].start_back()
-    for c in v_chip:
-        c.wait_recv()
-    total = vs[1]
-    for d in range(1, chips):
-        total = total + vgot[d]
-    vgot[chips + plane] = total
+    vgot[chips + plane] = vs[0] + vgot[0]
 
     def v_z(e, sender):
         return pltpu.make_async_remote_copy(
@@ -934,7 +993,16 @@
 
     for e in range(1, planes):
         v_z(e, plane).start()
-
+    for e in range(1, planes):
+        v_z(e, lax.rem(plane + planes - e, planes)).wait_recv()
+    total = vgot[chips]
+    for z in range(1, planes):
+        total = total + vgot[chips + z]
+    vs[1] = total
+    v_chip = [remote(vs.at[1], vgot.at[d], vsend.at[d], vrecv.at[d], lax.rem(f + 2 * d, F)) for d in range(1, chips)]
+    for c in v_chip:
+        c.start()
+    two[1].start_back()
     one_a.receive()
     one_b.receive()
     s_out = []
@@ -945,11 +1013,11 @@
         c.start()
         gq_ref[core, pr] = fin2[pr, pl.ds(pl.multiple_of(core * r, r), r), :]
         s_out.append(c)
-    for e in range(1, planes):
-        v_z(e, lax.rem(plane + planes - e, planes)).wait_recv()
-    total = vgot[chips]
-    for z in range(1, planes):
-        total = total + vgot[chips + z]
+    for c in v_chip:
+        c.wait_recv()
+    total = vs[1]
+    for d in range(1, chips):
+        total = total + vgot[d]
     vout_ref[...] = total
     for c in s_out:
         c.wait()

time: 197 us -> 183 us (0.929)
  Pallas kernels: 192 us -> 179 us
    pallas_call x1, Pallas kernels: 97.1 us -> 83.7 us  [last(): pl.pallas_call(functools.partial(last_kernel, F), out_shape=[jax.ShapeDty...]
where the time goes in v2:
time: 183 us
  Pallas kernels  179 us (98%)
  local copies, waits for them, and re-layouts  3.93 us (2%)
    pallas_call x1, Pallas kernels, first(): pl.pallas_call(functools.partial(first_kernel, F, n), out_shape=[jax.Shap...  90.9 us
    pallas_call x1, Pallas kernels, last(): pl.pallas_call(functools.partial(last_kernel, F), out_shape=[jax.ShapeDty...  83.7 us
    pallas_call x1, Pallas kernels, finish(): pl.pallas_call(finish_kernel, out_shape=[jax.ShapeDtypeStruct(lo.shape, b...  3.98 us

profile of v2, /device:TPU:0, one launch (start us, length us, event | category | flops | bytes accessed | tf_op | source)
XLA Modules:
  0.0 183.3 jit_solution(6737960165101551586)
XLA Ops:
  0.7 1.2 dynamic-slice_bitcast_fusion.parents_ref
  1.9 0.8 concatenate.3
  2.8 0.6 broadcast_in_dim.9.vec_ref
  3.4 90.9 %front.1 = (bf16[512,2560]{1,0:T(8,128)(2,1)}, bf16[20,128,512]{2,1,0:T(8,128)(2,1)}, bf16[20,128,256]{2,1,0:T(8,128)(2,1)}, bf16[256,2560]{1,0:T(8,128)(2,1)}, ...) custom-call(s32[16]{0:T(128)} %dynamic-slice_bitcast_fusion.parents_, ...), custom_call_target="tpu_custom_call" | custom-call | tf_op jit(solution)/shard_map/front/pallas_call | solution.py:683
  94.3 83.7 %back.1 = (bf16[2,640,512]{2,1,0:T(8,128)(2,1)}, bf16[2,640,512]{2,1,0:T(8,128)(2,1)}, bf16[2,2,64,384]{3,2,1,0:T(8,128)(2,1)}, bf16[256,512]{1,0:T(8,128)(2,1)}...) custom-call(s32[16]{0:T(128)} %dynamic-slice_bitcast_fusion.parents_ref, bf16[20,128,512]{2,1,0:T(8,128)(2,1)} %get-tuple-element.47.kaug_h, ...), custom_call_target="tpu_custom_call" | custom-call | tf_op jit(solution)/shard_map/back/pallas_call | solution.py:1072
  178.0 0.0 copy-start
  178.0 4.0 %finish.1 = (bf16[2,640,512]{2,1,0:T(8,128)(2,1)}, bf16[2,640,512]{2,1,0:T(8,128)(2,1)}, f32[64,512]{1,0:T(8,128)}, f32[64,512]{1,0:T(8,128)}, f32[64,512]{1,0:T...) custom-call(bf16[2,640,512]{2,1,0:T(8,128)(2,1)} %get-tuple-element.65.lo_in, ...), custom_call_target="tpu_custom_call" | custom-call | tf_op jit(solution)/shard_map/finish/pallas_call | solution.py:1106
  182.0 0.0 copy-done
  182.0 0.1 constant_dynamic-slice_fusion
  182.1 0.5 slice_bitcast_fusion.1
  182.6 0.6 dynamic_slice.11
  (4 shorter events, 0.0 us)
Async XLA Ops:
  178.0 4.0 %copy-start = (f32[16,512]{1,0:T(8,128)S(1)}, f32[16,512]{1,0:T(8,128)}, u32[]{:S(2)}) copy-start(f32[16,512]{1,0:T(8,128)} %get-tuple-element.72) | copy-start | bytes 98308
